TPU v7x, 128 devices: a whole 4x4x4 slice. The times are simulated.
128 devices in a mesh: row: 8 (over z_hi, y), col: 16 (over z_lo, x, core).
Axes of the slice: x: 4, y: 4, z: 4 (z_hi: 2, z_lo: 2; z = z_hi * 2 + z_lo), core: 2. Of those that a mesh axis runs over, the one named last changes fastest.
Arguments:
- node_features: bfloat16 [6144, 1024], P('row'), may hold values from -28 to 28
- edge_weight: bfloat16 [6144, 6144], P('row', 'col'), may hold values from -0.078125 to 0.078125
- pattern: int32 [48, 48], P('row', 'col'), may hold values from 0 to 1, as said below
- w_qkv: bfloat16 [1024, 3072], replicated, may hold values from -0.1875 to 0.1875
- w_out: bfloat16 [1024, 1024], P(None, 'col'), may hold values from -0.1875 to 0.1875
- bias_gain: float32 [16], replicated, may hold values from -2 to 2
- bias_rate: float32 [16], replicated, may hold values from 2 to 12
Outputs:
- mixed: bfloat16 [6144, 1024], P('row', 'col')
Inputs may be any that keep to these rules, and one draw needn't show every extreme that they name: pattern[i][i] is 1 for every i; the share of ones differs from block-row to block-row.
All inputs are finite; a program needn't handle non-finite values.
Results may differ from a plain program's by a relative error of at most 0.02.
Values may be sent and summed in bfloat16 or wider, within the bound.
A program may use at most 128 MiB of HBM per device.

v0:
```python
import math

import jax
import jax.numpy as jnp
from jax import lax
from jax.sharding import PartitionSpec as P

D = 1024
HEADS = 16
BLK = 128
SWEEPS = 3
HDIM = 64


def spread(value, axis, source):
    kept = jnp.where(lax.axis_index(axis) == source, value, 0).astype(value.dtype)
    return lax.psum(kept, axis)


def expand_blocks(pattern):
    block_rows, block_cols = pattern.shape
    grid = jnp.broadcast_to(pattern[:, None, :, None] > 0, (block_rows, BLK, block_cols, BLK))
    return grid.reshape(block_rows * BLK, block_cols * BLK)


def sweep(operator_panel, ranks, keep_mask, identity):
    product = jnp.dot(
        operator_panel,
        lax.all_gather(ranks.astype(jnp.bfloat16), "row", axis=0, tiled=True),
        preferred_element_type=jnp.float32,
    )
    return jnp.where(keep_mask, 0.15 * identity + 0.85 * product, jnp.zeros((), jnp.float32))


def shards(node_features, edge_weight, pattern, w_qkv, w_out, bias_gain, bias_rate):
    rows_here, cols_here = edge_weight.shape
    col_count = lax.axis_size("col")
    nodes_all = cols_here * col_count
    col_pos = lax.axis_index("col")
    keep_mask = expand_blocks(pattern)
    adjacency = jnp.where(keep_mask, edge_weight, jnp.zeros_like(edge_weight))
    row_ids = lax.axis_index("row") * rows_here + lax.iota(jnp.int32, rows_here)
    col_ids = col_pos * cols_here + lax.iota(jnp.int32, cols_here)
    identity = (row_ids[:, None] == col_ids[None, :]).astype(jnp.float32)
    ranks = jnp.where(
        keep_mask,
        0.15 * identity + 0.1275 * adjacency.astype(jnp.float32),
        jnp.zeros((), jnp.float32),
    )
    for sweep_index in range(SWEEPS - 1):
        operator_panel = lax.all_gather(adjacency, "col", axis=1, tiled=True)
        ranks = sweep(operator_panel, ranks, keep_mask, identity)
    w_query = w_qkv[:, :D]
    queries = jnp.dot(node_features, w_query, preferred_element_type=jnp.float32).astype(
        jnp.bfloat16
    )
    key_half = lax.dynamic_slice_in_dim(node_features, col_pos % 2 * cols_here, cols_here, 0)
    key_rows = spread(key_half, "row", col_pos // 2)
    keys_values = jnp.dot(key_rows, w_qkv[:, D:], preferred_element_type=jnp.float32).astype(
        jnp.bfloat16
    )
    query_heads = queries.reshape(rows_here, HEADS, HDIM)
    key_heads = keys_values[:, :D].reshape(cols_here, HEADS, HDIM)
    value_heads = keys_values[:, D:].reshape(cols_here, HEADS, HDIM)
    score_scale = 1.0 / math.sqrt(HDIM)
    root_nodes = math.sqrt(nodes_all)
    scores = (
        jnp.einsum("rhd,chd->hrc", query_heads, key_heads, preferred_element_type=jnp.float32)
        * score_scale
    )
    scores = scores + bias_gain[:, None, None] * jnp.tanh(
        bias_rate[:, None, None] * root_nodes * ranks[None]
    )
    masked = jnp.where(keep_mask[None], scores, -1e30)
    local_peak = jnp.max(masked, axis=2)
    row_peak = lax.pmax(local_peak.astype(jnp.bfloat16), "col").astype(local_peak.dtype)
    expo = jnp.where(
        keep_mask[None], jnp.exp(masked - row_peak[:, :, None]), jnp.zeros((), jnp.float32)
    )
    totals = jnp.sum(expo, axis=2).T
    numer = jnp.einsum(
        "hrc,chd->rhd", expo.astype(jnp.bfloat16), value_heads, preferred_element_type=jnp.float32
    )
    numer = numer.reshape(rows_here, D)
    numer_all, totals_all = (
        lax.psum(numer.astype(jnp.bfloat16), "col").astype(jnp.float32),
        lax.psum(totals.astype(jnp.bfloat16), "col").astype(jnp.float32),
    )
    attended = numer_all.reshape(rows_here, HEADS, HDIM) / totals_all[:, :, None]
    attended = attended.reshape(rows_here, D).astype(jnp.bfloat16)
    return jnp.dot(attended, w_out, preferred_element_type=jnp.float32).astype(jnp.bfloat16)


def solution(mesh):
    in_specs = (P("row", None), P("row", "col"), P("row", "col"), P(), P(None, "col"), P(), P())
    out_specs = P("row", "col")
    return jax.shard_map(shards, mesh=mesh, in_specs=in_specs, out_specs=out_specs, check_vma=False)
```

profile of v0, /device:TPU:1, one launch (start us, length us, event | category | flops | bytes accessed | tf_op | source)
XLA Modules:
  0.0 528.8 jit_solution(16860841790847176826)
XLA Ops:
  6.6 0.8 broadcast_compare_fusion
  7.4 0.2 broadcast_in_dim.49
  7.6 0.1 copy.27
  7.7 0.4 copy.21
  8.1 2.3 fusion.25
  10.4 0.0 all-gather.4.cloned.1.call-start
  10.5 1.0 broadcast_select_fusion
  11.5 0.0 all-reduce.3.cloned.1.call-start
  11.6 1.1 dynamic-slice_select_fusion
  12.7 0.0 all-gather.8.cloned.1.call-start
  12.7 76.2 %all-gather.6.cloned.1.call-done = bf16[6144,384]{1,0:T(8,128)(2,1)} async-done(((bf16[768,384]{1,0:T(8,128)(2,1)}), bf16[6144,384]{1,0:T(8,128)(2,1)}) %all-gather.6.cloned.1.call-update) | async-done | bytes 4718608 | tf_op jit(solution)/shard_map/all_gather | solution.py:29
  88.9 57.4 %all-gather.4.cloned.1.call-done = bf16[768,6144]{1,0:T(8,128)(2,1)} async-done(((bf16[768,384]{1,0:T(8,128)(2,1)}), bf16[768,6144]{1,0:T(8,128)(2,1)}) %all-gather.4.cloned.1.call-update) | async-done | bytes 9437200 | tf_op jit(solution)/shard_map/all_gather | solution.py:51
  146.4 9.7 %fusion.23 = bf16[768,384]{1,0:T(8,128)(2,1)} fusion(pred[768,384]{1,0:T(32,128)(4,1)S(1)} %copy.21, bf16[768,6144]{1,0:T(8,128)(2,1)} %all-gather.4.cloned.1.call-done, bf16[6144,384]{1,0:T(8,128)(2,1)} %all-gather.6.cloned.1.call-done, s32[384]{0:T(512)S(1)} %iota_add_fusion.1, s32[768]{0:T(1024)S(1)} %iota_add_fusion), kind=kOutput, calls=%fused_computation.24 | convolution fusion | flops 3625648128 | bytes 15045120 | tf_op jit(solution)/shard_map/dot_general | solution.py:27
  156.1 0.2 all-reduce.5.cloned.1.call-start
  156.4 3.9 fusion.15
  160.3 1.6 copy.16
  161.9 68.5 %all-reduce.3.cloned.1.call-done = bf16[384,1024]{1,0:T(8,128)(2,1)} async-done(((bf16[384,1024]{1,0:T(8,128)(2,1)}), bf16[384,1024]{1,0:T(8,128)(2,1)}) %all-reduce.3.cloned.1.call-update) | async-done | bytes 786448 | tf_op jit(solution)/shard_map/psum | solution.py:17
  230.4 4.2 fusion.10
  234.6 0.1 fusion.27
  234.8 1.2 copy.17
  235.9 0.4 copy.15
  236.3 75.1 %all-gather.8.cloned.1.call-done = bf16[6144,384]{1,0:T(8,128)(2,1)} async-done(((bf16[768,384]{1,0:T(8,128)(2,1)}), bf16[6144,384]{1,0:T(8,128)(2,1)}) %all-gather.8.cloned.1.call-update) | async-done | bytes 4718608 | tf_op jit(solution)/shard_map/all_gather | solution.py:29
  311.4 9.9 %fusion.22 = f32[768,384]{1,0:T(8,128)} fusion(pred[768,384]{1,0:T(32,128)(4,1)S(1)} %copy.21, bf16[768,6144]{1,0:T(8,128)(2,1)} %all-gather.4.cloned.1.call-done, bf16[6144,384]{1,0:T(8,128)(2,1)} %all-gather.8.cloned.1.call-done, s32[384]{0:T(512)S(1)} %iota_add_fusion.1, s32[768]{0:T(1024)S(1)} %iota_add_fusion), kind=kOutput, calls=%fused_computation.23 | convolution fusion | flops 3625353216 | bytes 15634944 | tf_op jit(solution)/shard_map/dot_general | solution.py:27
  321.2 2.7 copy.22
  323.9 12.0 %fusion.28 = (bf16[16,768]{1,0:T(8,128)(2,1)S(1)}, f32[16,768,384]{1,2,0:T(8,128)}) fusion(f32[768,384]{0,1:T(8,128)} %copy.22, f32[16]{0:T(128)S(1)} %broadcast_multiply_fusion, f32[16]{0:T(128)S(1)} %copy-done.5, bf16[768,16,64]{0,2,1:T(8,128)(2,1)S(1)} %bitcast.37, bf16[384,16,64]{0,2,1:T(8,128)(2,1)} %bitcast.39, pred[768,384]{0,1:T(8,128)(4,1)S(1)} %bitcast.33), kind=kOutput, calls=%fused_computation.38 | convolution fusion | flops 632279040 | bytes 22732928 | tf_op jit(solution)/shard_map/rhd,chd->hrc/dot_general | solution.py:68
  335.9 51.2 %pmax.7 = bf16[16,768]{1,0:T(8,128)(2,1)S(1)} all-reduce(bf16[16,768]{1,0:T(8,128)(2,1)S(1)} %get-tuple-element.7), channel_id=1, replica_groups=mesh['row'=8,'col'=16] {'col'}, use_global_device_ids=true, to_apply=%region_2.3 | all-reduce | flops 12288 | bytes 49152 | tf_op jit(solution)/shard_map/pmax | solution.py:76
  387.2 10.7 %fusion.18 = bf16[16,64,768]{2,1,0:T(8,128)(2,1)} fusion(bf16[384,16,64]{0,2,1:T(8,128)(2,1)S(1)} %bitcast.36, f32[16,768,384]{1,2,0:T(8,128)} %get-tuple-element.8, f32[16,768]{1,0:T(8,128)S(1)} %convert_element_type.60, pred[768,384]{0,1:T(8,128)(4,1)S(1)} %bitcast.34), kind=kOutput, calls=%fused_computation.19 | convolution fusion | flops 618921984 | bytes 21577728 | tf_op jit(solution)/shard_map/hrc,chd->rhd/dot_general | solution.py:81
  397.9 9.6 %fusion = bf16[16,768]{1,0:T(8,128)(2,1)S(1)} fusion(f32[16,768,384]{1,2,0:T(8,128)} %get-tuple-element.8, f32[16,768]{1,0:T(8,128)S(1)} %convert_element_type.60, pred[768,384]{0,1:T(8,128)(4,1)S(1)} %bitcast.35), kind=kLoop, calls=%fused_computation.2 | loop fusion | flops 14143488 | bytes 19243008 | tf_op jit(solution)/shard_map/reduce_sum | solution.py:80
  407.5 53.1 %psum.23 = bf16[768,16]{0,1:T(8,128)(2,1)S(1)} all-reduce(bf16[768,16]{0,1:T(8,128)(2,1)S(1)} %bitcast.40), channel_id=1, replica_groups=mesh['row'=8,'col'=16] {'col'}, use_global_device_ids=true, to_apply=%region_5.6 | all-reduce | flops 12288 | bytes 49152 | tf_op jit(solution)/shard_map/psum | solution.py:87
  460.6 58.9 %all-reduce.5.cloned.1.call-done = bf16[768,1024]{0,1:T(8,128)(2,1)} async-done(((bf16[768,1024]{0,1:T(8,128)(2,1)}), bf16[768,1024]{0,1:T(8,128)(2,1)}) %all-reduce.5.cloned.1.call-update) | async-done | bytes 1572880 | tf_op jit(solution)/shard_map/psum | solution.py:86
  519.5 1.7 fusion.9
  521.2 1.0 convolution_convert_fusion
  (23 shorter events, 0.1 us)
Async XLA Ops:
  6.5 514.7 %copy-start = (bf16[1024,64]{0,1:T(8,128)(2,1)S(1)}, bf16[1024,64]{0,1:T(8,128)(2,1)}, u32[]{:S(2)}) copy-start(bf16[1024,64]{0,1:T(8,128)(2,1)} %param.11) | copy-start | bytes 393220
  6.5 3.9 copy-start.1
  6.5 5.0 copy-start.3
  6.5 82.4 %all-gather.6.cloned.1.call-start = ((), (), s32[]{:S(2)}) async-start(), calls=%async_computation.2 | async-start | bytes 5308416 | tf_op jit(solution)/shard_map/all_gather | solution.py:29
  10.4 136.0 %all-gather.4.cloned.1.call-start = ((), (), s32[]{:S(2)}) async-start(), calls=%async_computation.1 | async-start | bytes 10027008 | tf_op jit(solution)/shard_map/all_gather | solution.py:51
  11.5 218.9 %all-reduce.3.cloned.1.call-start = ((), (), s32[]{:S(2)}) async-start(), calls=%async_computation | async-start | bytes 1572864 | tf_op jit(solution)/shard_map/psum | solution.py:17
  12.7 298.7 %all-gather.8.cloned.1.call-start = ((), (), s32[]{:S(2)}) async-start(), calls=%async_computation.3 | async-start | bytes 5308416 | tf_op jit(solution)/shard_map/all_gather | solution.py:29
  156.1 363.4 %all-reduce.5.cloned.1.call-start = ((), (), s32[]{:S(2)}) async-start(), calls=%async_computation.4 | async-start | bytes 3145728 | tf_op jit(solution)/shard_map/psum | solution.py:86
  160.3 1.6 copy-start.4
  236.3 87.6 %copy-start.2 = (bf16[768,1024]{0,1:T(8,128)(2,1)S(1)}, bf16[768,1024]{0,1:T(8,128)(2,1)}, u32[]{:S(2)}) copy-start(bf16[768,1024]{0,1:T(8,128)(2,1)} %copy.16) | copy-start | bytes 4718596
  236.3 87.6 %copy-start.5 = (f32[16]{0:T(128)S(1)}, f32[16]{0:T(128)}, u32[]{:S(2)}) copy-start(f32[16]{0:T(128)} %param.12) | copy-start | bytes 196
Sparse Core Ops, SparseCore 0:
  10.5 78.3 all-gather.5
  90.6 55.7 all-gather.3
  148.9 81.4 all-reduce.2
  232.6 78.7 all-gather.7
  398.1 121.4 all-reduce.4
where the time goes:
time: 529 us
  waiting for transfers between devices  336 us (64%)
  blocking collectives  104 us (20%)
  matrix products  51.5 us (10%)
  other arithmetic  16.5 us (3%)
  between operations  13.3 us (3%)
  local copies, waits for them, and re-layouts  6.66 us (1%)
    all_gather x2, waiting for transfers between devices, sweep(): lax.all_gather(ranks.astype(jnp.bfloat16), 'row', axis=0, tiled=True)  151 us
    psum x1, waiting for transfers between devices, spread(): return lax.psum(kept, axis)  68.5 us
    psum x1, waiting for transfers between devices, shards(): lax.psum(numer.astype(jnp.bfloat16), 'col').astype(jnp.float32)  58.9 us
    all_gather x1, waiting for transfers between devices, shards(): operator_panel = lax.all_gather(adjacency, 'col', axis=1, tiled=True)  57.4 us
    psum x1, blocking collectives, shards(): lax.psum(totals.astype(jnp.bfloat16), 'col').astype(jnp.float32)  53.1 us
    pmax x1, blocking collectives, shards(): lax.pmax(local_peak.astype(jnp.bfloat16), 'col').astype(local_peak.dtype)  51.2 us
    dot_general x2, matrix products, sweep(): jnp.dot(operator_panel, lax.all_gather(ranks.astype(jnp.bfloat16), 'row',...  19.6 us
    dot_general x1, matrix products, shards(): jnp.einsum('rhd,chd->hrc', query_heads, key_heads, preferred_element_type...  12 us
  transfers between devices with their start and end apart: 5, of which 5 were waited for; matrix products, arithmetic and copies ran while one was open for 6% of the time, Pallas kernels for 0%

commit v1 on v0

v1 whole, which is shorter than its diff:
```python
import math

import jax
import jax.numpy as jnp
from jax import lax
from jax.experimental import pallas as pl
from jax.experimental.pallas import tpu as pltpu
from jax.sharding import PartitionSpec as P

D = 1024
HEADS = 16
BLK = 128
HDIM = 64
NODES = 6144
ROWS = 768
HALF = 384
QC = 3
CLS = 4
PIECE = 32
LOG2E = 1.4426950408889634
BIG = 1e30
MESH = pl.DeviceIdType.MESH
F32 = jnp.float32
BF16 = jnp.bfloat16


class Place:
    def __init__(self):
        r = lax.axis_index("row")
        c = lax.axis_index("col")
        self.zh, self.y = r // 4, r % 4
        self.zl, self.x, self.core = c // 8, (c // 2) % 4, c % 2
        self.z = 2 * self.zh + self.zl

    def at(self, x=None, y=None, z=None, core=None):
        x = self.x if x is None else x
        y = self.y if y is None else y
        z = self.z if z is None else z
        core = self.core if core is None else core
        return ((z // 2) * 4 + y, ((z % 2) * 4 + x) * 2 + core)


def remote(src, dst, send, recv, device):
    return pltpu.make_async_remote_copy(
        src_ref=src, dst_ref=dst, send_sem=send, recv_sem=recv, device_id=device, device_id_type=MESH
    )


def greet(devices):
    barrier = pltpu.get_barrier_semaphore()
    for device in devices:
        pl.semaphore_signal(barrier, inc=1, device_id=device, device_id_type=MESH)
    pl.semaphore_wait(barrier, len(devices))


def ranks_kernel(
    adj, first, mask, feat, out, keys, panel, r1, r2, acc, staged, mrows,
    loc_sem, a_send, a_recv, on_send, on_recv, i_send, i_recv, m_send, m_recv,
    y_send, y_recv, s_send, s_recv, f_send, f_recv, o_send, o_recv,
):
    me = Place()
    x, y, z, zh, zl, core = me.x, me.y, me.z, me.zh, me.zl, me.core
    sibling = me.at(core=1 - core)
    far = (z + 2) % 4
    ring = {
        "x+": me.at(x=(x + 1) % 4), "x-": me.at(x=(x + 3) % 4),
        "y+": me.at(y=(y + 1) % 4), "y-": me.at(y=(y + 3) % 4),
        "z+": me.at(z=(z + 1) % 4), "z-": me.at(z=(z + 3) % 4),
    }
    turned = (zl * 4 + x, (zh * 4 + y) * 2 + core)
    turned_self = (zl == zh) & (x == y)
    friends = [sibling, *ring.values(), me.at(z=far, core=0), me.at(z=far, core=1)]
    barrier = pltpu.get_barrier_semaphore()
    for device in friends:
        pl.semaphore_signal(barrier, inc=1, device_id=device, device_id_type=MESH)

    @pl.when(jnp.logical_not(turned_self))
    def _():
        pl.semaphore_signal(barrier, inc=1, device_id=turned, device_id_type=MESH)

    pl.semaphore_wait(barrier, len(friends) + jnp.where(turned_self, 0, 1))

    sends = []

    def own(who):
        return panel.at[:, z, pl.ds(x * 3, 3), :, pl.ds(pl.multiple_of(who * 128, 128), 128)]

    here = pltpu.make_async_copy(adj.at[pl.ds(core * 12, 12)], own(core), loc_sem.at[0])
    here.start()
    over = remote(adj.at[pl.ds((1 - core) * 12, 12)], own(core), on_send.at[0], on_recv.at[0], sibling)
    over.start()
    sends.append(over)

    goal = 2 * core + zl
    for half in range(2):
        is_self = (core == zh) & (core == half)

        @pl.when(is_self)
        def _(half=half):
            pltpu.make_async_copy(first.at[half], r1.at[y, zh, :, half], i_recv.at[zh]).start()
            pltpu.make_async_copy(mask, mrows.at[zh], m_recv.at[zh]).start()

        @pl.when(jnp.logical_not(is_self))
        def _(half=half):
            target = me.at(z=goal, core=half)
            remote(first.at[half], r1.at[y, zh, :, half], i_send.at[half], i_recv.at[zh], target).start()
            remote(mask, mrows.at[zh], m_send.at[half], m_recv.at[zh], target).start()

    def key_half(who):
        return keys.at[pl.ds(pl.multiple_of(who * HALF, HALF), HALF)]

    my_rows = feat.at[pl.ds(pl.multiple_of(core * HALF, HALF), HALF)]

    @pl.when(turned_self)
    def _():
        pltpu.make_async_copy(my_rows, key_half(core), f_recv.at[0]).start()

    @pl.when(jnp.logical_not(turned_self))
    def _():
        remote(my_rows, key_half(core), f_send.at[0], f_recv.at[0], turned).start()

    here.wait()
    over.wait_recv()

    def a_step(q, cls, stage, arriving):
        sign = 1 if cls % 2 == 0 else -1
        mark = "+" if sign == 1 else "-"
        x_first = cls < 2
        short = stage < 3
        step = stage % 3
        along_x = x_first == short
        device = ring[("x" if along_x else "z") + mark]
        qc = q * CLS + cls

        def region(hop):
            if along_x:
                at_x = (x - sign * hop + 8) % 4
                if short:
                    return panel.at[qc, z, pl.ds(at_x * 3, 3)]
                return panel.at[qc, :, pl.ds(at_x * 3, 3)]
            at_z = (z - sign * hop + 8) % 4
            if short:
                return panel.at[qc, at_z, pl.ds(x * 3, 3)]
            return panel.at[qc, at_z]

        n = (q * CLS + cls) * 6 + stage
        ref = region(step + 1 if arriving else step)
        return remote(ref, ref, a_send.at[n], a_recv.at[n], device)

    def a_stage(q, stage):
        for cls in range(CLS):
            if stage > 0:
                a_step(q, cls, stage - 1, True).wait_recv()
            if stage < 6:
                send = a_step(q, cls, stage, False)
                send.start()
                sends.append(send)

    def y_step(base, cut, a, step, arriving):
        sign = 1 if a == 0 else -1
        n = base * 6 + a * 3 + step
        ref = cut((y - sign * (step + 1 if arriving else step) + 8) % 4, a, core)
        return remote(ref, ref, y_send.at[n], y_recv.at[n], ring["y+" if a == 0 else "y-"])

    def y_share(base, cut, a, step, arriving):
        sign = 1 if a == 0 else -1
        n = base * 8 + a * 4 + step
        ref = cut((y - sign * step + 8) % 4, a, 1 - core if arriving else core)
        return remote(ref, ref, s_send.at[n], s_recv.at[n], sibling)

    def y_stage(base, cut, step):
        for a in range(2):
            if step > 0:
                y_step(base, cut, a, step - 1, True).wait_recv()
            go = [y_step(base, cut, a, step, False)] if step < 3 else []
            for send in go + [y_share(base, cut, a, step, False)]:
                send.start()
                sends.append(send)

    def y_done(base, cut):
        for a in range(2):
            for step in range(4):
                y_share(base, cut, a, step, True).wait_recv()

    def cut1(at_y, a, who):
        return r1.at[at_y, a, :, who]

    def cut2(q):
        return lambda at_y, a, who: r2.at[at_y, a, q, who]

    def lhs(q, m, h, kc):
        top = panel[pl.ds(q * CLS, CLS), h, m * 3 + kc].reshape(BLK, 256)
        low = panel[pl.ds(q * CLS, CLS), 2 + h, m * 3 + kc].reshape(BLK, 256)
        return jnp.concatenate([top, low], axis=0)

    def diag(a, q):
        row = lax.broadcasted_iota(jnp.int32, (BLK, HALF), 0) + q * BLK
        col = lax.broadcasted_iota(jnp.int32, (BLK, HALF), 1)
        own_block = (zl == a) & (y == x) & (core == zh)
        return jnp.where((row == col) & own_block, F32(0.15), F32(0.0))

    def keep_row(a, q):
        return mrows[a, pl.ds(core * 3 + q, 1), :] > 0.5

    def sweep_one(q):
        def body(m, total):
            for h in range(2):
                for kc in range(3):
                    rhs = r1[m, h, kc].reshape(256, HALF)
                    total = total + jnp.dot(lhs(q, m, h, kc), rhs, preferred_element_type=F32)
            return total

        total = lax.fori_loop(0, 4, body, jnp.zeros((2 * BLK, HALF), F32))
        for a in range(2):
            value = diag(a, q) + 0.85 * total[a * BLK:(a + 1) * BLK]
            r2[y, a, q, core] = jnp.where(keep_row(a, q), value, 0.0).astype(BF16)

    def sweep_two(rows, kc, start):
        def body(m, _):
            for q in rows:
                total = None
                for h in range(2):
                    part = jnp.dot(lhs(q, m, h, kc), r2[m, h, kc].reshape(256, HALF), preferred_element_type=F32)
                    total = part if total is None else total + part
                acc[q] = acc[q] + total
            return 0

        if start:
            for q in rows:
                acc[q] = jnp.zeros((2 * BLK, HALF), F32)
        lax.fori_loop(0, 4, body, 0)

    events = []
    order = 0

    def plan(when, what):
        nonlocal order
        events.append((when, order, what))
        order += 1

    def start_ranks():
        for a in range(2):
            pltpu.make_async_copy(first.at[0], r1.at[y, a, :, core], i_recv.at[a]).wait()
        y_stage(0, cut1, 0)

    def share_keys():
        pltpu.make_async_copy(my_rows, key_half(core), f_recv.at[0]).wait()
        share = remote(key_half(core), key_half(core), f_send.at[1], f_recv.at[1], sibling)
        share.start()
        sends.append(share)

    plan(4.0, start_ranks)
    for step in range(1, 4):
        plan(4.0 + 7.0 * step, lambda step=step: y_stage(0, cut1, step))
    plan(20.0, share_keys)
    for q in range(QC):
        base = 3.0 + 14.0 * q
        for stage in range(7):
            when = base + (2.6 * stage if stage < 3 else 8.0 + 5.0 * (stage - 3))
            plan(when, lambda q=q, stage=stage: a_stage(q, stage))
        full = base + 23.0

        def first_sweep(q=q):
            if q == 0:
                y_done(0, cut1)
                for a in range(2):
                    pltpu.make_async_copy(mask, mrows.at[a], m_recv.at[a]).wait()
            sweep_one(q)
            y_stage(1 + q, cut2(q), 0)

        plan(max(full, 26.0) + 0.1, first_sweep)
        for step in range(1, 4):
            plan(full + 1.5 + 3.6 * step, lambda q=q, step=step: y_stage(1 + q, cut2(q), step))
        plan(full + 12.5, lambda q=q: y_done(1 + q, cut2(q)))
        if q == 0:
            plan(full + 14.2, lambda: sweep_two((0, 1), 0, True))
        if q == 1:
            plan(full + 14.2, lambda: sweep_two((2,), 0, True))
            plan(full + 14.3, lambda: sweep_two((0, 1, 2), 1, False))
        if q == 2:
            plan(full + 14.2, lambda: sweep_two((0, 1, 2), 2, False))
    for _, _, what in sorted(events, key=lambda e: e[:2]):
        what()

    for q in range(QC):
        for a in range(2):
            value = diag(a, q) + 0.85 * acc[q, a * BLK:(a + 1) * BLK]
            staged[a, q] = jnp.where(keep_row(a, q), value, F32(BIG)).astype(BF16)
    mine = pltpu.make_async_copy(staged.at[zh], out.at[zh], loc_sem.at[1])
    mine.start()
    swap = remote(staged.at[1 - zh], out.at[zh], o_send.at[0], o_recv.at[0], me.at(z=far))
    swap.start()
    mine.wait()
    swap.wait_recv()
    swap.wait_send()
    remote(key_half(1 - core), key_half(1 - core), f_send.at[1], f_recv.at[1], sibling).wait_recv()
    for send in sends:
        send.wait_send()
    for half in range(2):
        @pl.when(jnp.logical_not((core == zh) & (core == half)))
        def _(half=half):
            target = me.at(z=goal, core=half)
            remote(first.at[half], r1.at[y, zh, :, half], i_send.at[half], i_recv.at[zh], target).wait_send()
            remote(mask, mrows.at[zh], m_send.at[half], m_recv.at[zh], target).wait_send()

    @pl.when(jnp.logical_not(turned_self))
    def _():
        remote(my_rows, key_half(core), f_send.at[0], f_recv.at[0], turned).wait_send()


def ranks_call(adj, first, mask, feat):
    dma = pltpu.SemaphoreType.DMA
    anywhere = pl.BlockSpec(memory_space=pl.ANY)
    vmem = pl.BlockSpec(memory_space=pltpu.VMEM)
    return pl.pallas_call(
        ranks_kernel,
        name="ranks",
        out_shape=(
            jax.ShapeDtypeStruct((2, QC, BLK, HALF), BF16),
            jax.ShapeDtypeStruct((ROWS, D), BF16),
        ),
        in_specs=[anywhere] * 4,
        out_specs=(vmem, vmem),
        scratch_shapes=[
            pltpu.VMEM((QC * CLS, 4, 12, PIECE, 256), BF16),
            pltpu.VMEM((4, 2, 3, 2, BLK, HALF), BF16),
            pltpu.VMEM((4, 2, 3, 2, BLK, HALF), BF16),
            pltpu.VMEM((QC, 2 * BLK, HALF), F32),
            pltpu.VMEM((2, QC, BLK, HALF), BF16),
            pltpu.VMEM((2, 8, HALF), F32),
            dma((2,)),
            dma((QC * CLS * 6,)), dma((QC * CLS * 6,)),
            dma((1,)), dma((1,)),
            dma((2,)), dma((2,)),
            dma((2,)), dma((2,)),
            dma((24,)), dma((24,)),
            dma((32,)), dma((32,)),
            dma((2,)), dma((2,)),
            dma((1,)), dma((1,)),
        ],
        compiler_params=pltpu.CompilerParams(
            collective_id=0, has_side_effects=True, vmem_limit_bytes=48 * 1024 * 1024
        ),
    )(adj, first, mask, feat)


def attend_kernel(
    ranks, query, keys_t, values, w_out, gain, rate, out,
    bias_in, hide, numer, numer_all, stats, stats_all, att, att_all, w_both, mix,
    n_send, n_recv, t_send, t_recv, g_send, g_recv, w_send, w_recv, x_send, x_recv,
):
    me = Place()
    core = me.core
    sibling = me.at(core=1 - core)
    spot = me.zl * 4 + me.x

    def chip(k):
        other = (spot + k) % 8
        return other, me.at(x=other % 4, z=2 * me.zh + other // 4)

    greet([sibling] + [chip(k)[1] for k in range(1, 8)])
    sends = []
    w_copy = remote(w_out, w_both, w_send, w_recv, sibling)
    w_copy.start()
    sends.append(w_copy)

    for half in range(2):
        for q in range(QC):
            value = ranks[half, q].astype(F32)
            rows, cols = pl.ds(q * BLK, BLK), pl.ds(half * HALF, HALF)
            bias_in[rows, cols] = value * math.sqrt(NODES)
            hide[rows, cols] = jnp.where(value < 1e20, F32(0.0), F32(-BIG))

    lane = lax.broadcasted_iota(jnp.int32, (BLK, BLK), 1)

    def block(pair, row):
        cols = pl.ds(pl.multiple_of(pair * BLK, BLK), BLK)
        rows = pl.ds(pl.multiple_of(row * BLK, BLK), BLK)
        q2 = query[rows, cols]
        k2 = keys_t[cols, :]
        v2 = values[:, cols]
        spread = bias_in[rows, :]
        away = hide[rows, :]
        both = []
        kept = stats[rows, :]
        for side in range(2):
            head = pair * 2 + side
            q1 = jnp.where(lane // HDIM == side, q2, jnp.zeros_like(q2))
            s = jnp.dot(q1, k2, preferred_element_type=F32) * F32(LOG2E / math.sqrt(HDIM)) + away
            top = jnp.maximum(jnp.max(s, axis=1, keepdims=True), F32(-1e29))
            bias = (gain[head] * F32(LOG2E)) * jnp.tanh(spread * rate[head])
            e = jnp.exp2((s - top) + bias)
            total = jnp.sum(e, axis=1, keepdims=True)
            both.append(jnp.dot(e.astype(BF16), v2, preferred_element_type=F32))
            kept = jnp.where(lane == head, total, jnp.where(lane == HEADS + head, top, kept))
        stats[rows, :] = kept
        numer[rows, cols] = jnp.where(lane < HDIM, both[0], both[1]).astype(BF16)

    stats[...] = jnp.zeros_like(stats)

    def part(ref, row, g):
        return ref.at[pl.ds(pl.multiple_of(row * 48, 16), 48), pl.ds(g * 256, 256)]

    for g in range(4):
        def body(t, _, g=g):
            block(g * 2 + t // QC, t % QC)
            return 0

        lax.fori_loop(0, 2 * QC, body, 0)
        for k in range(1, 8):
            other, device = chip(k)
            n = g * 8 + k
            copy = remote(
                part(numer, other, g), numer_all.at[spot, :, pl.ds(g * 256, 256)],
                n_send.at[n], n_recv.at[n], device,
            )
            copy.start()
            sends.append(copy)
    for k in range(1, 8):
        other, device = chip(k)
        copy = remote(
            stats.at[pl.ds(pl.multiple_of(other * 48, 16), 48)], stats_all.at[spot],
            t_send.at[k], t_recv.at[k], device,
        )
        copy.start()
        sends.append(copy)

    own_rows = pl.ds(pl.multiple_of(spot * 48, 16), 48)
    stats_all[spot] = stats[own_rows, :]
    numer_all[spot] = numer[own_rows, :]
    for k in range(1, 8):
        source = (spot + 8 - k) % 8
        remote(stats_all.at[source], stats_all.at[source], t_send.at[k], t_recv.at[k], sibling).wait_recv()
        for g in range(4):
            ref = numer_all.at[source, :, pl.ds(g * 256, 256)]
            remote(ref, ref, n_send.at[g * 8 + k], n_recv.at[g * 8 + k], sibling).wait_recv()

    table = [stats_all[s] for s in range(8)]
    tops = [t[:, HEADS:2 * HEADS] for t in table]
    peak = tops[0]
    for t in tops[1:]:
        peak = jnp.maximum(peak, t)
    weights = [jnp.exp2(t - peak) for t in tops]
    total = weights[0] * table[0][:, :HEADS]
    for s in range(1, 8):
        total = total + weights[s] * table[s][:, :HEADS]
    weights = [w / total for w in weights]
    for pair in range(HEADS // 2):
        cols = pl.ds(pair * BLK, BLK)
        low = lax.broadcasted_iota(jnp.int32, (48, BLK), 1) < HDIM
        value = jnp.zeros((48, BLK), F32)
        for s in range(8):
            w = jnp.where(low, weights[s][:, 2 * pair:2 * pair + 1], weights[s][:, 2 * pair + 1:2 * pair + 2])
            value = value + w * numer_all[s, :, cols].astype(F32)
        att[:, cols] = value.astype(BF16)

    for k in range(1, 8):
        _, device = chip(k)
        copy = remote(att, att_all.at[spot], g_send.at[k], g_recv.at[k], device)
        copy.start()
        sends.append(copy)
    att_all[spot] = att[...]
    for k in range(1, 8):
        ref = att_all.at[(spot + 8 - k) % 8]
        remote(ref, ref, g_send.at[k], g_recv.at[k], sibling).wait_recv()
    w_copy.wait_recv()
    gathered = att_all[...].reshape(HALF, D)
    mix[...] = jnp.dot(gathered, w_both[...], preferred_element_type=F32).astype(BF16)
    there = remote(mix, out.at[core], x_send, x_recv, sibling)
    there.start()
    sends.append(there)
    out[core] = jnp.dot(gathered, w_out[...], preferred_element_type=F32).astype(BF16)
    remote(mix, out.at[1 - core], x_send, x_recv, sibling).wait_recv()
    for send in sends:
        send.wait_send()


def attend_call(ranks, query, keys_t, values, w_out, gain, rate):
    dma = pltpu.SemaphoreType.DMA
    vmem = pl.BlockSpec(memory_space=pltpu.VMEM)
    smem = pl.BlockSpec(memory_space=pltpu.SMEM)
    return pl.pallas_call(
        attend_kernel,
        name="attend",
        out_shape=jax.ShapeDtypeStruct((2, HALF, HDIM), BF16),
        in_specs=[vmem] * 5 + [smem] * 2,
        out_specs=vmem,
        scratch_shapes=[
            pltpu.VMEM((HALF, ROWS), F32),
            pltpu.VMEM((HALF, ROWS), F32),
            pltpu.VMEM((HALF, D), BF16),
            pltpu.VMEM((8, 48, D), BF16),
            pltpu.VMEM((HALF, BLK), F32),
            pltpu.VMEM((8, 48, BLK), F32),
            pltpu.VMEM((48, D), BF16),
            pltpu.VMEM((8, 48, D), BF16),
            pltpu.VMEM((D, HDIM), BF16),
            pltpu.VMEM((HALF, HDIM), BF16),
            dma((32,)), dma((32,)),
            dma((8,)), dma((8,)),
            dma((8,)), dma((8,)),
            dma, dma,
            dma, dma,
        ],
        compiler_params=pltpu.CompilerParams(
            collective_id=1, has_side_effects=True, vmem_limit_bytes=48 * 1024 * 1024
        ),
    )(ranks, query, keys_t, values, w_out, gain, rate)


def prepare(edge_weight, pattern):
    rows_here, cols_here = edge_weight.shape
    blocks = pattern > 0
    grid = jnp.broadcast_to(blocks[:, None, :, None], (rows_here // BLK, BLK, cols_here // BLK, BLK))
    keep = grid.reshape(rows_here, cols_here)
    adjacency = jnp.where(keep, edge_weight, jnp.zeros_like(edge_weight))
    row_ids = lax.axis_index("row") * rows_here + lax.iota(jnp.int32, rows_here)
    col_ids = lax.axis_index("col") * cols_here + lax.iota(jnp.int32, cols_here)
    identity = (row_ids[:, None] == col_ids[None, :]).astype(F32)
    first = jnp.where(keep, 0.15 * identity + 0.1275 * adjacency.astype(F32), F32(0.0)).astype(BF16)
    panel = adjacency.reshape(2 * QC * CLS, PIECE, 3, BLK).transpose(0, 2, 1, 3)
    mask = jnp.broadcast_to(blocks[:, :, None], (6, 3, BLK)).reshape(6, cols_here).astype(F32)
    return panel, first.reshape(2, QC, BLK, cols_here), jnp.pad(mask, ((0, 2), (0, 0)))


def shards(node_features, edge_weight, pattern, w_qkv, w_out, bias_gain, bias_rate):
    panel, first, mask = prepare(edge_weight, pattern)
    ranks, keys = ranks_call(panel, first, mask, node_features)
    core = lax.axis_index("col") % 2
    mine = lax.dynamic_slice_in_dim(node_features, core * HALF, HALF, 0)
    query = jnp.dot(mine, w_qkv[:, :D], preferred_element_type=F32).astype(BF16)
    keys_t = lax.dot_general(
        w_qkv[:, D:2 * D], keys, (((0,), (1,)), ((), ())), preferred_element_type=F32
    ).astype(BF16)
    values = jnp.dot(keys, w_qkv[:, 2 * D:], preferred_element_type=F32).astype(BF16)
    mixed = attend_call(ranks, query, keys_t, values, w_out, bias_gain, bias_rate)
    return mixed.reshape(2 * HALF, HDIM)


def solution(mesh):
    in_specs = (P("row", None), P("row", "col"), P("row", "col"), P(), P(None, "col"), P(), P())
    return jax.shard_map(shards, mesh=mesh, in_specs=in_specs, out_specs=P("row", "col"), check_vma=False)
```

time: 529 us -> 213 us (0.40)
  waiting for transfers between devices: 336 us -> 0 us
  Pallas kernels: 0 us -> 190 us
  blocking collectives: 104 us -> 0 us
  matrix products: 51.5 us -> 10.5 us
  other arithmetic: 16.5 us -> 2.07 us
  between operations: 13.3 us -> 0.19 us
    all_gather x3 -> x0, waiting for transfers between devices: 209 us -> none  [the longest x2 151 us: sweep(): lax.all_gather(ranks.astype(jnp.bfloat16), 'row', axis=0, tiled=True)]
    pallas_call x0 -> x2, Pallas kernels: none -> 190 us  [the longest x1 144 us: ranks_call(): pl.pallas_call(ranks_kernel, name='ranks', out_shape=(jax.ShapeDtypeStruc...]
    psum x2 -> x0, waiting for transfers between devices: 127 us -> none  [the longest x1 68.5 us: spread(): return lax.psum(kept, axis)]
    psum x1 -> x0, blocking collectives: 53.1 us -> none  [shards(): lax.psum(totals.astype(jnp.bfloat16), 'col').astype(jnp.float32)]
    pmax x1 -> x0, blocking collectives: 51.2 us -> none  [shards(): lax.pmax(local_peak.astype(jnp.bfloat16), 'col').astype(local_peak.dtype)]
    dot_general x7 -> x3, matrix products: 51.5 us -> 10.5 us  [the longest x1 3.56 us: shards(): query = jnp.dot(mine, w_qkv[:, :D], preferred_element_type=F32).astype(BF16)]
    reduce_sum x1 -> x0, other arithmetic: 9.58 us -> none  [shards(): totals = jnp.sum(expo, axis=2).T]
    unnamed x13 -> x24, local copies, waits for them, and re-layouts: 0.18 us -> 6.42 us
  transfers between devices with their start and end apart: 5 -> 0, of which waited for: 5 -> 0; matrix products, arithmetic and copies ran while one was open for 6% -> 0% of each run, Pallas kernels for 0% -> 0%
where the time goes in v1:
time: 213 us
  Pallas kernels  190 us (89%)
  matrix products  10.5 us (5%)
  local copies, waits for them, and re-layouts  10.4 us (5%)
    pallas_call x1, Pallas kernels, ranks_call(): pl.pallas_call(ranks_kernel, name='ranks', out_shape=(jax.ShapeDtypeStruc...  144 us
    pallas_call x1, Pallas kernels, attend_call(): pl.pallas_call(attend_kernel, name='attend', out_shape=jax.ShapeDtypeStru...  45.4 us
    unnamed x24, local copies, waits for them, and re-layouts  6.42 us

profile of v1, /device:TPU:1, one launch (start us, length us, event | category | flops | bytes accessed | tf_op | source)
XLA Modules:
  0.0 212.8 jit_solution(81872740245030049)
XLA Ops:
  0.0 1.3 copy.13
  1.3 0.7 fusion.20
  2.0 0.2 broadcast_in_dim.7
  2.2 0.2 bitcast_select_fusion
  2.3 0.3 copy.14
  2.6 0.2 reshape.25
  2.9 0.1 copy.30
  3.0 0.0 copy-start
  3.0 1.2 select_convert_fusion
  4.2 1.4 copy.16
  5.6 0.1 copy.17
  5.7 0.1 broadcast_bitcast_fusion
  5.8 0.0 copy-done
  5.8 144.2 %ranks.1 = (bf16[2,3,128,384]{3,2,1,0:T(8,128)(2,1)S(1)}, bf16[768,1024]{1,0:T(8,128)(2,1)S(1)}) custom-call(bf16[24,3,32,128]{3,2,1,0:T(8,128)(2,1)S(1)} %bitcast.24, bf16[2,3,128,384]{3,2,1,0:T(8,128)(2,1)S(1)} %bitcast.23, f32[8,384]{1,0:T(8,128)S(1)} %pad.4.mask, bf16[768,1024]{1,0:T(8,128)(2,1)S(1)} %copy-done), custom_call_target="tpu_custom_call" | custom-call | tf_op jit(solution)/shard_map/ranks/pallas_call | solution.py:315
  150.0 0.0 copy-start.3
  150.0 0.8 copy-done.3
  150.8 1.1 copy-done.7
  152.0 3.6 %fusion.15.query = bf16[384,1024]{1,0:T(8,128)(2,1)} fusion(bf16[1024,3072]{1,0:T(8,128)(2,1)} %param.10, bf16[768,1024]{1,0:T(8,128)(2,1)S(1)} %copy-done, s32[]{:T(128)S(6)} %select_n.21), kind=kOutput, calls=%fused_computation.9 | convolution fusion | flops 805699584 | bytes 3670020 | tf_op jit(solution)/shard_map/dot_general | solution.py:531
  155.5 0.0 copy-done.8
  155.5 3.5 %fusion.12.keys_t = bf16[1024,768]{1,0:T(8,128)(2,1)S(1)} fusion(bf16[768,1024]{1,0:T(8,128)(2,1)S(1)} %copy-done.8, bf16[1024,3072]{1,0:T(8,128)(2,1)} %param.10), kind=kOutput, calls=%fused_computation.8 | convolution fusion | flops 1611399168 | bytes 5242880 | tf_op jit(solution)/shard_map/dot_general | solution.py:532
  159.0 0.0 copy-start.9
  159.1 0.0 copy-start.5
  159.1 0.0 copy-start.6
  159.1 3.5 %fusion.9.values = bf16[768,1024]{1,0:T(8,128)(2,1)S(1)} fusion(bf16[768,1024]{1,0:T(8,128)(2,1)S(1)} %copy-done.8, bf16[1024,3072]{1,0:T(8,128)(2,1)} %param.10), kind=kOutput, calls=%fused_computation.7 | convolution fusion | flops 1611399168 | bytes 5242880 | tf_op jit(solution)/shard_map/dot_general | solution.py:535
  162.5 0.0 copy-done.9
  162.5 0.2 copy.19.w_out
  162.7 0.0 copy-done.5
  162.8 1.1 copy-done.2
  163.9 1.1 copy-done.4
  164.9 45.4 %attend.1 = bf16[2,384,64]{2,1,0:T(8,128)(2,1)S(1)} custom-call(bf16[2,3,128,384]{3,2,1,0:T(8,128)(2,1)S(1)} %copy-done.4, bf16[384,1024]{1,0:T(8,128)(2,1)S(1)} %copy-done.2, bf16[1024,768]{1,0:T(8,128)(2,1)S(1)} %fusion.12.keys_t, bf16[768,1024]{1,0:T(8,128)(2,1)S(1)} %fusion.9.values, bf16[1024,64]{1,0:T(8,128)(2,1)S(1)} %copy.19.w_out, f32[16]{0:T(128)S(1)} %copy-done.5, ...), custom_call_target="tpu_custom_call" | custom-call | tf_op jit(solution)/shard_map/attend/pallas_call | solution.py:482
  210.4 0.7 copy-done.1
  211.1 1.7 copy.20
  (10 shorter events, 0.0 us)
Async XLA Ops:
  3.0 2.8 %copy-start = (bf16[768,1024]{1,0:T(8,128)(2,1)S(1)}, bf16[768,1024]{1,0:T(8,128)(2,1)}, u32[]{:S(2)}) copy-start(bf16[768,1024]{1,0:T(8,128)(2,1)} %feat.1) | copy-start | bytes 4718596
  150.0 0.8 copy-start.3
  150.8 1.2 copy-start.7
  152.0 3.6 %copy-start.8 = (bf16[768,1024]{1,0:T(8,128)(2,1)S(1)}, bf16[768,1024]{1,0:T(8,128)(2,1)}, u32[]{:S(2)}) copy-start(bf16[768,1024]{1,0:T(8,128)(2,1)} %copy-done.7) | copy-start | bytes 4718596
  159.0 3.5 %copy-start.9 = (bf16[1024,64]{0,1:T(8,128)(2,1)S(1)}, bf16[1024,64]{0,1:T(8,128)(2,1)}, u32[]{:S(2)}) copy-start(bf16[1024,64]{0,1:T(8,128)(2,1)} %param.11) | copy-start | bytes 393220
  159.1 3.7 %copy-start.5 = (f32[16]{0:T(128)S(1)}, f32[16]{0:T(128)}, u32[]{:S(2)}) copy-start(f32[16]{0:T(128)} %gain.1) | copy-start | bytes 196
  159.1 3.7 %copy-start.6 = (f32[16]{0:T(128)S(1)}, f32[16]{0:T(128)}, u32[]{:S(2)}) copy-start(f32[16]{0:T(128)} %rate.1) | copy-start | bytes 196
  162.7 1.1 copy-start.2
  163.9 1.1 copy-start.4
  210.4 0.7 copy-start.1

commit v2 on v0

v2 whole, which is shorter than its diff:
```python
import math

import jax
import jax.numpy as jnp
from jax import lax
from jax.experimental import pallas as pl
from jax.experimental.pallas import tpu as pltpu
from jax.sharding import PartitionSpec as P

D = 1024
HEADS = 16
BLK = 128
HDIM = 64
NODES = 6144
ROWS = 768
HALF = 384
QC = 3
CHUNKS = 6
CLS = 4
PIECE = 16
KEYROWS = 48
LOG2E = 1.4426950408889634
BIG = 1e30
MESH = pl.DeviceIdType.MESH
F32 = jnp.float32
BF16 = jnp.bfloat16


class Place:
    def __init__(self):
        r = lax.axis_index("row")
        c = lax.axis_index("col")
        self.zh, self.y = r // 4, r % 4
        self.zl, self.x, self.core = c // 8, (c // 2) % 4, c % 2
        self.z = 2 * self.zh + self.zl

    def at(self, x=None, y=None, z=None, core=None):
        x = self.x if x is None else x
        y = self.y if y is None else y
        z = self.z if z is None else z
        core = self.core if core is None else core
        return ((z // 2) * 4 + y, ((z % 2) * 4 + x) * 2 + core)


def remote(src, dst, send, recv, device):
    return pltpu.make_async_remote_copy(
        src_ref=src, dst_ref=dst, send_sem=send, recv_sem=recv, device_id=device, device_id_type=MESH
    )


def fused_kernel(
    edge, pattern, feat, w_qkv, w_out_t, gain, rate, out,
    panel, r1, r2, acc, staged, landed, adj, first, mrows, mboth, keys, own_feat, w_all, edge_v,
    query, key_proj, value_proj, scores, bias_in, numer, numer_all, stats, stats_all, att, w_cols, mix,
    loc_sem, a_send, a_recv, on_send, on_recv, i_send, i_recv, m_send, m_recv,
    y_send, y_recv, s_send, s_recv, f_send, f_recv, o_send, o_recv,
    n_send, n_recv, t_send, t_recv, w_send, w_recv, x_send, x_recv,
):
    me = Place()
    x, y, z, zh, zl, core = me.x, me.y, me.z, me.zh, me.zl, me.core
    sibling = me.at(core=1 - core)
    far = (z + 2) % 4
    spot = zl * 4 + x
    ring = {
        "x+": me.at(x=(x + 1) % 4), "x-": me.at(x=(x + 3) % 4),
        "z+": me.at(z=(z + 1) % 4), "z-": me.at(z=(z + 3) % 4),
    }
    turned = (zl * 4 + x, (zh * 4 + y) * 2 + core)
    turned_self = (zl == zh) & (x == y)

    def chip(k, who=None):
        other = (spot + k) % 8
        return other, me.at(x=other % 4, z=2 * zh + other // 4, core=who)

    def y_peer(k):
        return me.at(y=(y + k) % 4)

    friends = [sibling, me.at(z=(z + 2 * zl + 3) % 4), me.at(z=far, core=0), me.at(z=far, core=1)]
    friends += [y_peer(k) for k in (1, 2, 3)]
    friends += [chip(k, who)[1] for k in range(1, 8) for who in (core, 1 - core)]
    barrier = pltpu.get_barrier_semaphore()
    for device in friends:
        pl.semaphore_signal(barrier, inc=1, device_id=device, device_id_type=MESH)

    @pl.when(jnp.logical_not(turned_self))
    def _():
        pl.semaphore_signal(barrier, inc=1, device_id=turned, device_id_type=MESH)

    sends = []

    def go(copy):
        copy.start()
        sends.append(copy)

    loads = {
        "edge": pltpu.make_async_copy(edge, edge_v, loc_sem.at[0]),
        "feat": pltpu.make_async_copy(
            feat.at[pl.ds(pl.multiple_of(core * HALF, HALF), HALF)], own_feat, loc_sem.at[1]
        ),
        "w": pltpu.make_async_copy(w_qkv, w_all, loc_sem.at[2]),
    }
    for load in loads.values():
        load.start()
    loads["edge"].wait()

    same = (zl * 4 + x == zh * 4 + y)
    for rb in range(6):
        for cb in range(3):
            on = jnp.where(pattern[rb, cb] > 0, F32(1.0), F32(0.0))
            kept = edge_v[pl.ds(rb * BLK, BLK), pl.ds(cb * BLK, BLK)] * on.astype(BF16)
            adj[pl.ds(rb * 8, 8), cb] = kept.reshape(8, PIECE, BLK)
            row = lax.broadcasted_iota(jnp.int32, (BLK, BLK), 0) + rb * BLK
            col = lax.broadcasted_iota(jnp.int32, (BLK, BLK), 1) + cb * BLK + core * HALF
            diagonal = jnp.where((row == col) & same, F32(0.15), F32(0.0))
            value = (diagonal + F32(0.1275) * kept.astype(F32)) * on
            first[rb // 3, rb % 3, :, pl.ds(cb * BLK, BLK)] = value.astype(BF16)
            mboth[core, pl.ds(rb, 1), pl.ds(cb * BLK, BLK)] = jnp.full((1, BLK), on, F32)
    mask = mboth.at[core]

    pl.semaphore_wait(barrier, len(friends) + jnp.where(turned_self, 0, 1))

    def own(who):
        return panel.at[:, z, pl.ds(x * 3, 3), :, pl.ds(pl.multiple_of(who * 128, 128), 128)]

    rows24 = CHUNKS * CLS
    here = pltpu.make_async_copy(adj.at[pl.ds(core * rows24, rows24)], own(core), loc_sem.at[3])
    here.start()
    over = remote(adj.at[pl.ds((1 - core) * rows24, rows24)], own(core), on_send.at[0], on_recv.at[0], sibling)
    go(over)

    goal = 2 * core + zl
    for half in range(2):
        is_self = (core == zh) & (core == half)

        @pl.when(is_self)
        def _(half=half):
            pltpu.make_async_copy(first.at[half], r1.at[y, zh, :, half], i_recv.at[zh]).start()
            pltpu.make_async_copy(mask, mrows.at[zh], m_recv.at[zh]).start()

        @pl.when(jnp.logical_not(is_self))
        def _(half=half):
            target = me.at(z=goal, core=half)
            remote(first.at[half], r1.at[y, zh, :, half], i_send.at[half], i_recv.at[zh], target).start()
            remote(mask, mrows.at[zh], m_send.at[half], m_recv.at[zh], target).start()

    go(remote(mask, mask, on_send.at[1], on_recv.at[1], sibling))

    mine = pl.ds(pl.multiple_of(spot * 2 * KEYROWS + core * KEYROWS, KEYROWS), KEYROWS)

    @pl.when(turned_self)
    def _():
        pltpu.make_async_copy(feat.at[mine], keys.at[zh, y, core], f_recv.at[0]).start()

    @pl.when(jnp.logical_not(turned_self))
    def _():
        remote(feat.at[mine], keys.at[zl, x, core], f_send.at[0], f_recv.at[0], turned).start()

    here.wait()
    over.wait_recv()

    def a_copy(j, cls, leg, kind, arriving):
        sign = 1 if cls % 2 == 0 else -1
        along_x = (cls < 2) == (leg == 0)
        head = sign if kind != 1 else -sign
        device = ring[("x" if along_x else "z") + ("+" if head == 1 else "-")]
        hop = {0: 0, 1: 0, 2: -sign}[kind] - (head if arriving else 0)
        jc = j * CLS + cls
        if along_x:
            at_x = (x + hop + 8) % 4
            cols = pl.ds(at_x * 3, 3)
            ref = panel.at[jc, z, cols] if leg == 0 else panel.at[jc, :, cols]
        else:
            at_z = (z + hop + 8) % 4
            ref = panel.at[jc, at_z, pl.ds(x * 3, 3)] if leg == 0 else panel.at[jc, at_z]
        n = jc * 6 + leg * 3 + kind
        return remote(ref, ref, a_send.at[n], a_recv.at[n], device)

    def a_stage(j, stage):
        for cls in range(CLS):
            if stage in (1, 3):
                leg = stage // 2
                a_copy(j, cls, leg, 0, True).wait_recv()
                go(a_copy(j, cls, leg, 2, False))
            else:
                if stage > 0:
                    a_copy(j, cls, stage // 2 - 1, 1, True).wait_recv()
                    a_copy(j, cls, stage // 2 - 1, 2, True).wait_recv()
                if stage < 4:
                    go(a_copy(j, cls, stage // 2, 0, False))
                    go(a_copy(j, cls, stage // 2, 1, False))

    def y_copy(base, cut, k, arriving):
        ref = cut((y - k + 4) % 4 if arriving else y, core)
        n = base * 3 + k - 1
        return remote(ref, ref, y_send.at[n], y_recv.at[n], y_peer(k))

    def y_share(base, cut, k, arriving):
        ref = cut((y - k + 4) % 4, 1 - core if arriving else core)
        n = base * 4 + k
        return remote(ref, ref, s_send.at[n], s_recv.at[n], sibling)

    def y_begin(base, cut):
        for k in (1, 3, 2):
            go(y_copy(base, cut, k, False))
        go(y_share(base, cut, 0, False))

    def y_pass(base, cut, k):
        y_copy(base, cut, k, True).wait_recv()
        go(y_share(base, cut, k, False))

    def y_done(base, cut):
        for k in range(4):
            y_share(base, cut, k, True).wait_recv()

    def cut1(at_y, who):
        return r1.at[at_y, :, :, who]

    def cut2(q):
        return lambda at_y, who: r2.at[at_y, :, q, who]

    def cutk(at_y, who):
        return keys.at[:, at_y, who]

    def lhs(q, m, h, kc):
        top = panel[pl.ds(q * 8, 8), h, m * 3 + kc].reshape(BLK, 256)
        low = panel[pl.ds(q * 8, 8), 2 + h, m * 3 + kc].reshape(BLK, 256)
        return jnp.concatenate([top, low], axis=0)

    def diag(a, q):
        row = lax.broadcasted_iota(jnp.int32, (BLK, HALF), 0) + q * BLK
        col = lax.broadcasted_iota(jnp.int32, (BLK, HALF), 1)
        own_block = (zl == a) & (y == x) & (core == zh)
        return jnp.where((row == col) & own_block, F32(0.15), F32(0.0))

    def masked_ranks(a, q, total):
        keep = mrows[a, pl.ds(core * 3 + q, 1), :] > 0.5
        return jnp.where(keep, diag(a, q) + 0.85 * total, 0.0).astype(BF16)

    def sweep_one(q):
        def body(m, total):
            for h in range(2):
                for kc in range(3):
                    rhs = r1[m, h, kc].reshape(256, HALF)
                    total = total + jnp.dot(lhs(q, m, h, kc), rhs, preferred_element_type=F32)
            return total

        total = lax.fori_loop(0, 4, body, jnp.zeros((2 * BLK, HALF), F32))
        for a in range(2):
            r2[y, a, q, core] = masked_ranks(a, q, total[a * BLK:(a + 1) * BLK])

    def sweep_two(rows, kc, start):
        def body(m, _):
            for q in rows:
                total = None
                for h in range(2):
                    part = jnp.dot(lhs(q, m, h, kc), r2[m, h, kc].reshape(256, HALF), preferred_element_type=F32)
                    total = part if total is None else total + part
                acc[q] = acc[q] + total
            return 0

        if start:
            for q in rows:
                acc[q] = jnp.zeros((2 * BLK, HALF), F32)
        lax.fori_loop(0, 4, body, 0)

    def project(dst, src, first_col, n):
        def body(t, _):
            cols = pl.ds(pl.multiple_of(t * 256, 256), 256)
            w = w_all[:, pl.ds(pl.multiple_of(first_col + t * 256, 256), 256)]
            dst[:, cols] = jnp.dot(src, w, preferred_element_type=F32).astype(BF16)
            return 0

        lax.fori_loop(n, n + 1, body, 0)

    lane = lax.broadcasted_iota(jnp.int32, (BLK, BLK), 1)

    def score_block(t):
        pair, row = t // QC, t % QC
        cols = pl.ds(pl.multiple_of(pair * BLK, BLK), BLK)
        rows = pl.ds(pl.multiple_of(row * BLK, BLK), BLK)
        q2 = query[rows, cols]
        k2 = key_proj[:, cols]
        away = [jnp.where(mboth[c, pl.ds(core * 3 + row, 1), :] > 0.5, F32(0.0), F32(-BIG)) for c in range(2)]
        away = jnp.concatenate(away, axis=1)
        kept = stats[rows, :]
        for side in range(2):
            head = pair * 2 + side
            q1 = jnp.where(lane // HDIM == side, q2, jnp.zeros_like(q2))
            s = lax.dot_general(q1, k2, (((1,), (1,)), ((), ())), preferred_element_type=F32)
            s = s * F32(LOG2E / math.sqrt(HDIM)) + away
            top = jnp.maximum(jnp.max(s, axis=1, keepdims=True), F32(-1e29))
            scores[head, rows, :] = s - top
            kept = jnp.where(lane == HEADS + head, top, kept)
        stats[rows, :] = kept

    def score_blocks(low, high):
        def body(t, _):
            score_block(t)
            return 0

        lax.fori_loop(low, high, body, 0)

    def expo_block(t):
        pair, row = t // QC, t % QC
        cols = pl.ds(pl.multiple_of(pair * BLK, BLK), BLK)
        rows = pl.ds(pl.multiple_of(row * BLK, BLK), BLK)
        v2 = value_proj[:, cols]
        spread = bias_in[rows, :]
        both = []
        kept = stats[rows, :]
        for side in range(2):
            head = pair * 2 + side
            bias = (gain[head] * F32(LOG2E)) * jnp.tanh(spread * rate[head])
            e = jnp.exp2(scores[head, rows, :] + bias)
            kept = jnp.where(lane == head, jnp.sum(e, axis=1, keepdims=True), kept)
            both.append(jnp.dot(e.astype(BF16), v2, preferred_element_type=F32))
        stats[rows, :] = kept
        numer[rows, cols] = jnp.where(lane < HDIM, both[0], both[1]).astype(BF16)

    events = []

    def plan(when, what):
        events.append((when, len(events), what))

    def load_weights():
        loads["feat"].wait()
        loads["w"].wait()
        stats[...] = jnp.zeros_like(stats)

    def begin_ranks():
        for a in range(2):
            pltpu.make_async_copy(first.at[0], r1.at[y, a, :, core], i_recv.at[a]).wait()
        y_begin(0, cut1)

    def begin_keys():
        pltpu.make_async_copy(feat.at[mine], keys.at[zh, y, core], f_recv.at[0]).wait()
        ref = keys.at[zh, y, core]
        go(remote(ref, ref, f_send.at[1], f_recv.at[1], me.at(z=far)))

    def spread_keys():
        ref = keys.at[1 - zh, y, core]
        remote(ref, ref, f_send.at[1], f_recv.at[1], me.at(z=far)).wait_recv()
        y_begin(4, cutk)

    plan(7.0, load_weights)
    for n in range(4):
        plan(7.5 + 0.1 * n, lambda n=n: project(query, own_feat[...], 0, n))
    plan(9.0, begin_ranks)
    for k, when in ((1, 26.0), (3, 26.0), (2, 35.0)):
        plan(when, lambda k=k: y_pass(0, cut1, k))
    plan(10.0, begin_keys)
    plan(14.0, spread_keys)
    for k, when in ((1, 24.0), (3, 24.0), (2, 25.0)):
        plan(when, lambda k=k: y_pass(4, cutk, k))
    plan(27.0, lambda: y_done(4, cutk))
    for n in range(4):
        plan(27.5 + n, lambda n=n: project(key_proj, keys[...].reshape(ROWS, D), D, n))
        plan(31.5 + n, lambda n=n: project(value_proj, keys[...].reshape(ROWS, D), 2 * D, n))
    for j in range(CHUNKS):
        long = 13.0 + 7.9 * j
        for stage, when in enumerate((6.0 + 0.8 * j, 9.0 + 0.8 * j, long, long + 6.0, long + 13.0)):
            plan(when, lambda j=j, stage=stage: a_stage(j, stage))

    def ready():
        y_done(0, cut1)
        for a in range(2):
            pltpu.make_async_copy(mask, mrows.at[a], m_recv.at[a]).wait()

    plan(35.9, lambda: remote(mask, mboth.at[1 - core], on_send.at[1], on_recv.at[1], sibling).wait_recv())
    for n in range(8):
        plan(36.0 + 3.2 * n, lambda n=n: score_blocks(3 * n, 3 * n + 3))
    plan(38.4, ready)
    for q, when in enumerate((38.5, 50.0, 65.7)):
        def first_sweep(q=q):
            sweep_one(q)
            y_begin(1 + q, cut2(q))

        plan(when, first_sweep)
        for k, late in ((1, 5.0), (3, 5.0), (2, 6.0)):
            plan(when + late, lambda q=q, k=k: y_pass(1 + q, cut2(q), k))
        plan(when + 8.0, lambda q=q: y_done(1 + q, cut2(q)))
    plan(50.5, lambda: sweep_two((0, 1), 0, True))
    plan(59.0, lambda: sweep_two((0, 1), 1, False))
    plan(66.0, lambda: sweep_two((2,), 0, True))
    plan(66.1, lambda: sweep_two((2,), 1, False))
    plan(74.0, lambda: sweep_two((0, 1, 2), 2, False))

    def send_weights():
        for k in range(8):
            _, device = chip(k, 1 - core if k == 0 else None)
            go(remote(w_out_t, w_cols.at[spot, core], w_send.at[k], w_recv.at[k], device))
        pltpu.make_async_copy(w_out_t, w_cols.at[spot, core], loc_sem.at[4]).start()

    plan(66.2, send_weights)
    for _, _, what in sorted(events, key=lambda e: e[:2]):
        what()

    for a in range(2):
        for q in range(QC):
            staged[a, q] = masked_ranks(a, q, acc[q, a * BLK:(a + 1) * BLK])
    swap = remote(staged.at[1 - zh], landed, o_send.at[0], o_recv.at[0], me.at(z=far))
    go(swap)

    pltpu.make_async_copy(w_out_t, w_cols.at[spot, core], loc_sem.at[4]).wait()
    for k in range(1, 8):
        source = (spot + 8 - k) % 8
        ref = w_cols.at[source, core]
        remote(ref, ref, w_send.at[k], w_recv.at[k], sibling).wait_recv()
        go(remote(ref, ref, w_send.at[7 + k], w_recv.at[7 + k], sibling))

    def widen(ref, half):
        for q in range(QC):
            cols = pl.ds(pl.multiple_of(half * HALF, HALF), HALF)
            bias_in[pl.ds(q * BLK, BLK), cols] = ref[q].astype(F32) * F32(math.sqrt(NODES))

    widen(staged.at[zh], zh)
    swap.wait_recv()
    widen(landed, 1 - zh)

    def part(ref, row, g):
        return ref.at[pl.ds(pl.multiple_of(row * KEYROWS, KEYROWS), KEYROWS), pl.ds(g * 256, 256)]

    for g in range(4):
        def body(t, _, g=g):
            expo_block(g * 2 * QC + t)
            return 0

        lax.fori_loop(0, 2 * QC, body, 0)
        for k in range(1, 8):
            other, device = chip(k)
            n = g * 8 + k
            dst = numer_all.at[spot, :, pl.ds(g * 256, 256)]
            go(remote(part(numer, other, g), dst, n_send.at[n], n_recv.at[n], device))
    for k in range(1, 8):
        other, device = chip(k)
        rows = stats.at[pl.ds(pl.multiple_of(other * KEYROWS, KEYROWS), KEYROWS)]
        go(remote(rows, stats_all.at[spot], t_send.at[k], t_recv.at[k], device))

    own_rows = pl.ds(pl.multiple_of(spot * KEYROWS, KEYROWS), KEYROWS)
    stats_all[spot] = stats[own_rows, :]
    numer_all[spot] = numer[own_rows, :]
    for k in range(1, 8):
        source = (spot + 8 - k) % 8
        remote(stats_all.at[source], stats_all.at[source], t_send.at[k], t_recv.at[k], sibling).wait_recv()
        for g in range(4):
            ref = numer_all.at[source, :, pl.ds(g * 256, 256)]
            remote(ref, ref, n_send.at[g * 8 + k], n_recv.at[g * 8 + k], sibling).wait_recv()

    table = [stats_all[s] for s in range(8)]
    tops = [t[:, HEADS:2 * HEADS] for t in table]
    peak = tops[0]
    for t in tops[1:]:
        peak = jnp.maximum(peak, t)
    weights = [jnp.exp2(t - peak) for t in tops]
    total = weights[0] * table[0][:, :HEADS]
    for s in range(1, 8):
        total = total + weights[s] * table[s][:, :HEADS]
    weights = [w / total for w in weights]
    low = lax.broadcasted_iota(jnp.int32, (KEYROWS, BLK), 1) < HDIM
    for pair in range(HEADS // 2):
        cols = pl.ds(pair * BLK, BLK)
        value = jnp.zeros((KEYROWS, BLK), F32)
        for s in range(8):
            w = jnp.where(low, weights[s][:, 2 * pair:2 * pair + 1], weights[s][:, 2 * pair + 1:2 * pair + 2])
            value = value + w * numer_all[s, :, cols].astype(F32)
        att[:, cols] = value.astype(BF16)

    for k in range(8):
        ref = w_cols.at[(spot + 8 - k) % 8, 1 - core]
        n = 0 if k == 0 else 7 + k
        remote(ref, ref, w_send.at[n], w_recv.at[n], sibling).wait_recv()
    mixed = lax.dot_general(
        att[...], w_cols[...].reshape(D, D), (((1,), (1,)), ((), ())), preferred_element_type=F32
    ).astype(BF16)
    for c in range(2 * 8):
        mix[c // 2, c % 2] = mixed[:, c * HDIM:(c + 1) * HDIM]

    def rows_of(who, at):
        return out.at[pl.ds(pl.multiple_of(who * HALF + at * KEYROWS, KEYROWS), KEYROWS)]

    for k in range(8):
        for flip in range(2):
            if k == 0 and flip == 0:
                continue
            other, device = chip(k, (core + flip) % 2)
            n = k * 2 + flip
            go(remote(mix.at[other, (core + flip) % 2], rows_of(core, spot), x_send.at[n], x_recv.at[n], device))
    last = pltpu.make_async_copy(mix.at[spot, core], rows_of(core, spot), loc_sem.at[5])
    last.start()
    for k in range(8):
        for flip in range(2):
            if k == 0 and flip == 0:
                continue
            ref = rows_of((core + flip) % 2, (spot + 8 - k) % 8)
            remote(ref, ref, x_send.at[k * 2 + flip], x_recv.at[k * 2 + flip], sibling).wait_recv()
    last.wait()
    for send in sends:
        send.wait_send()
    for half in range(2):
        @pl.when(jnp.logical_not((core == zh) & (core == half)))
        def _(half=half):
            target = me.at(z=goal, core=half)
            remote(first.at[half], r1.at[y, zh, :, half], i_send.at[half], i_recv.at[zh], target).wait_send()
            remote(mask, mrows.at[zh], m_send.at[half], m_recv.at[zh], target).wait_send()

    @pl.when(jnp.logical_not(turned_self))
    def _():
        remote(feat.at[mine], keys.at[zl, x, core], f_send.at[0], f_recv.at[0], turned).wait_send()


def shards(node_features, edge_weight, pattern, w_qkv, w_out, bias_gain, bias_rate):
    dma = pltpu.SemaphoreType.DMA
    anywhere = pl.BlockSpec(memory_space=pl.ANY)
    vmem = pl.BlockSpec(memory_space=pltpu.VMEM)
    smem = pl.BlockSpec(memory_space=pltpu.SMEM)
    pairs = [6 * CHUNKS * CLS, 2, 2, 2, 15, 20, 2, 1, 32, 8, 15, 16]
    sems = [dma((n,)) for n in pairs for _ in range(2)]
    return pl.pallas_call(
        fused_kernel,
        name="fused",
        out_shape=jax.ShapeDtypeStruct((ROWS, HDIM), BF16),
        in_specs=[anywhere, smem, anywhere, anywhere, anywhere, smem, smem],
        out_specs=vmem,
        scratch_shapes=[
            pltpu.VMEM((CHUNKS * CLS, 4, 12, PIECE, 256), BF16),
            pltpu.VMEM((4, 2, QC, 2, BLK, HALF), BF16),
            pltpu.VMEM((4, 2, QC, 2, BLK, HALF), BF16),
            pltpu.VMEM((QC, 2 * BLK, HALF), F32),
            pltpu.VMEM((2, QC, BLK, HALF), BF16),
            pltpu.VMEM((QC, BLK, HALF), BF16),
            pltpu.VMEM((2 * CHUNKS * CLS, 3, PIECE, BLK), BF16),
            pltpu.VMEM((2, QC, BLK, HALF), BF16),
            pltpu.VMEM((2, 8, HALF), F32),
            pltpu.VMEM((2, 8, HALF), F32),
            pltpu.VMEM((2, 4, 2, KEYROWS, D), BF16),
            pltpu.VMEM((HALF, D), BF16),
            pltpu.VMEM((D, 3 * D), BF16),
            pltpu.VMEM((ROWS, HALF), BF16),
            pltpu.VMEM((HALF, D), BF16),
            pltpu.VMEM((ROWS, D), BF16),
            pltpu.VMEM((ROWS, D), BF16),
            pltpu.VMEM((HEADS, HALF, ROWS), F32),
            pltpu.VMEM((HALF, ROWS), F32),
            pltpu.VMEM((HALF, D), BF16),
            pltpu.VMEM((8, KEYROWS, D), BF16),
            pltpu.VMEM((HALF, BLK), F32),
            pltpu.VMEM((8, KEYROWS, BLK), F32),
            pltpu.VMEM((KEYROWS, D), BF16),
            pltpu.VMEM((8, 2, HDIM, D), BF16),
            pltpu.VMEM((8, 2, KEYROWS, HDIM), BF16),
            dma((6,)),
            *sems,
        ],
        compiler_params=pltpu.CompilerParams(
            collective_id=0, has_side_effects=True, vmem_limit_bytes=65 * 1000 * 1000
        ),
    )(edge_weight, pattern, node_features, w_qkv, w_out.T, bias_gain, bias_rate)


def solution(mesh):
    in_specs = (P("row", None), P("row", "col"), P("row", "col"), P(), P(None, "col"), P(), P())
    return jax.shard_map(shards, mesh=mesh, in_specs=in_specs, out_specs=P("row", "col"), check_vma=False)
```

time: 529 us -> 160 us (0.30)
  waiting for transfers between devices: 336 us -> 0 us
  Pallas kernels: 0 us -> 157 us
  blocking collectives: 104 us -> 0 us
  matrix products: 51.5 us -> 0 us
  other arithmetic: 16.5 us -> 0 us
  between operations: 13.3 us -> 0.01 us
    all_gather x3 -> x0, waiting for transfers between devices: 209 us -> none  [the longest x2 151 us: sweep(): lax.all_gather(ranks.astype(jnp.bfloat16), 'row', axis=0, tiled=True)]
    pallas_call x0 -> x1, Pallas kernels: none -> 157 us  [shards(): pl.pallas_call(fused_kernel, name='fused', out_shape=jax.ShapeDtypeStruct...]
    psum x2 -> x0, waiting for transfers between devices: 127 us -> none  [the longest x1 68.5 us: spread(): return lax.psum(kept, axis)]
    psum x1 -> x0, blocking collectives: 53.1 us -> none  [shards(): lax.psum(totals.astype(jnp.bfloat16), 'col').astype(jnp.float32)]
    dot_general x7 -> x0, matrix products: 51.5 us -> none  [the longest x2 19.6 us: sweep(): jnp.dot(operator_panel, lax.all_gather(ranks.astype(jnp.bfloat16), 'row',...]
    pmax x1 -> x0, blocking collectives: 51.2 us -> none  [shards(): lax.pmax(local_peak.astype(jnp.bfloat16), 'col').astype(local_peak.dtype)]
    reduce_sum x1 -> x0, other arithmetic: 9.58 us -> none  [shards(): totals = jnp.sum(expo, axis=2).T]
  transfers between devices with their start and end apart: 5 -> 0, of which waited for: 5 -> 0; matrix products, arithmetic and copies ran while one was open for 6% -> 0% of each run, Pallas kernels for 0% -> 0%
where the time goes in v2:
time: 160 us
  Pallas kernels  157 us (98%)
  local copies, waits for them, and re-layouts  3.04 us (2%)
    pallas_call x1, Pallas kernels, shards(): pl.pallas_call(fused_kernel, name='fused', out_shape=jax.ShapeDtypeStruct...  157 us

profile of v2, /device:TPU:1, one launch (start us, length us, event | category | flops | bytes accessed | tf_op | source)
XLA Modules:
  0.0 159.9 jit_solution(17895222942616049813)
XLA Ops:
  0.0 1.4 copy.8.pattern
  1.4 156.9 %fused.1 = bf16[768,64]{1,0:T(8,128)(2,1)} custom-call(bf16[768,384]{1,0:T(8,128)(2,1)} %edge.1, s32[6,3]{1,0:T(8,128)} %copy.8.pattern, bf16[768,1024]{1,0:T(8,128)(2,1)} %feat.1, bf16[1024,3072]{1,0:T(8,128)(2,1)} %w_qkv.1, bf16[64,1024]{1,0:T(8,128)(2,1)} %bitcast.1, f32[16]{0:T(128)} %gain.1, f32[16]{0:T(128)} %rate.1), custom_call_target="tpu_custom_call" | custom-call | tf_op jit(solution)/shard_map/fused/pallas_call | solution.py:518
  158.2 1.7 %copy.9 = bf16[768,64]{0,1:T(8,128)(2,1)} copy(bf16[768,64]{1,0:T(8,128)(2,1)} %fused.1) | data formatting | bytes 196608 | tf_op jit(solution)/shard_map/fused/pallas_call | solution.py:518

commit v3 on v2

v3 whole, which is shorter than its diff:
```python
import math

import jax
import jax.numpy as jnp
from jax import lax
from jax.experimental import pallas as pl
from jax.experimental.pallas import tpu as pltpu
from jax.sharding import PartitionSpec as P

D = 1024
HEADS = 16
BLK = 128
HDIM = 64
NODES = 6144
ROWS = 768
HALF = 384
QC = 3
CHUNKS = 6
CLS = 4
X_FIRST = (2, 2, 2, 2, 2, 2)
RELAYED = ()
T_LOAD = 2.9
T_QUERY = (4.5, 3.5, 3.0, 4.0)
T_KEY = (27.5, 26.5, 25.0, 27.0)
T_VALUE = (29.5, 28.0, 33.5, 29.0)
T_FIRST = 0.0
T_OWN = (5.0, 11.5, 12.0, 13.5)
T_FAR = (5.5, 16.0, 15.5, 18.5)
T_FEAT = (2.5, 7.0, 21.5, 21.0, 23.5, 24.5)
T_PANEL = (
    (0.5, 1.0, 1.5, 2.0, 9.0, 10.0),
    (6.0, 6.5, 7.5, 8.0, 13.0, 14.5),
    (8.5, 9.5, 10.5, 11.0, 18.0, 20.5),
    (12.5, 14.0, 16.5, 17.0, 24.0, 28.5),
    (17.5, 19.5, 22.0, 22.5, 30.0, 34.0),
)
T_SCORE = (35.5, 36.0, 37.0, 38.5, 39.0, 41.0, 42.5, 43.5, 44.0, 44.5, 45.0, 46.0)
T_READY = 19.0
T_ONE = (
    (1, 0, (0, 128), 20.0), (2, 1, (0, 128), 23.0), (3, 2, (0, 64), 31.0), (6, 2, (64, 64), 34.5)
)
T_LATE = {
    1: (26.0, 25.5, 30.5, 31.5),
    2: (32.5, 33.0, 36.5, 39.5),
    3: (38.0, 37.5, 40.5, 43.0),
    6: (42.0, 41.5, 45.5, 46.5),
}
T_TWO = (((0, 1), 0, True, 32.0), ((2,), 0, True, 35.0), ((0, 1, 2), 1, False, 40.0))
FAMILY = (0, 1, 1, 1, 2, 0, 1)
PIECE = 16
KEYROWS = 48
OWNROWS = 16
LOG2E = 1.4426950408889634
BIG = 1e30
MESH = pl.DeviceIdType.MESH
F32 = jnp.float32
BF16 = jnp.bfloat16


class Place:
    def __init__(self):
        r = lax.axis_index("row")
        c = lax.axis_index("col")
        self.zh, self.y = r // 4, r % 4
        self.zl, self.x, self.core = c // 8, (c // 2) % 4, c % 2
        self.z = 2 * self.zh + self.zl

    def at(self, x=None, y=None, z=None, core=None):
        x = self.x if x is None else x
        y = self.y if y is None else y
        z = self.z if z is None else z
        core = self.core if core is None else core
        return ((z // 2) * 4 + y, ((z % 2) * 4 + x) * 2 + core)


def remote(src, dst, send, recv, device):
    return pltpu.make_async_remote_copy(
        src_ref=src, dst_ref=dst, send_sem=send, recv_sem=recv, device_id=device, device_id_type=MESH
    )


def fused_kernel(
    edge, pattern, feat, w_qkv, w_out_t, gain, rate, out,
    panel, r1, r2, acc, staged, landed, adj, first, mrows, mboth, keys, own_feat, w_all, edge_v,
    query, key_proj, value_proj, scores, bias_in, numer, numer_all, stats, stats_all, att, w_cols, mix,
    loc_sem, a_send, a_recv, on_send, on_recv, i_send, i_recv, m_send, m_recv,
    y_send, y_recv, s_send, s_recv, f_send, f_recv, o_send, o_recv,
    n_send, n_recv, t_send, t_recv, w_send, w_recv, x_send, x_recv,
):
    me = Place()
    x, y, z, zh, zl, core = me.x, me.y, me.z, me.zh, me.zl, me.core
    sibling = me.at(core=1 - core)
    spot = zl * 4 + x
    ring = {
        "x+": me.at(x=(x + 1) % 4), "x-": me.at(x=(x + 3) % 4),
        "z+": me.at(z=(z + 1) % 4), "z-": me.at(z=(z + 3) % 4),
    }
    turned = (zl * 4 + x, (zh * 4 + y) * 2 + core)
    turned_self = (zl == zh) & (x == y)

    def chip(k, who=None):
        other = (spot + k) % 8
        return other, me.at(x=other % 4, z=2 * zh + other // 4, core=who)

    def y_peer(k):
        return me.at(y=(y + k) % 4)

    cross = (z + 2 * zl + 3) % 4
    friends = [sibling, me.at(z=cross, core=0), me.at(z=cross, core=1)]
    friends += [((1 - zl) * 4 + x, (zh * 4 + y) * 2 + core), (zl * 4 + x, ((1 - zh) * 4 + y) * 2 + core)]
    friends += [y_peer(k) for k in (1, 2, 3)]
    friends += [chip(k, who)[1] for k in range(1, 8) for who in (core, 1 - core)]
    barrier = pltpu.get_barrier_semaphore()
    for device in friends:
        pl.semaphore_signal(barrier, inc=1, device_id=device, device_id_type=MESH)

    @pl.when(jnp.logical_not(turned_self))
    def _():
        pl.semaphore_signal(barrier, inc=1, device_id=turned, device_id_type=MESH)

    sends = []

    def go(copy):
        copy.start()
        sends.append(copy)

    def arrived(ref, sem):
        pltpu.make_async_copy(ref, ref, sem).wait()

    loads = {
        "edge": pltpu.make_async_copy(edge, edge_v, loc_sem.at[0]),
        "feat": pltpu.make_async_copy(
            feat.at[pl.ds(pl.multiple_of(core * HALF, HALF), HALF)], own_feat, loc_sem.at[1]
        ),
        "w": pltpu.make_async_copy(w_qkv, w_all, loc_sem.at[2]),
    }
    for load in loads.values():
        load.start()
    loads["edge"].wait()

    same = (zl * 4 + x == zh * 4 + y)
    for rb in range(6):
        for cb in range(3):
            on = jnp.where(pattern[cb, rb] > 0, F32(1.0), F32(0.0))
            kept = edge_v[pl.ds(rb * BLK, BLK), pl.ds(cb * BLK, BLK)] * on.astype(BF16)
            adj[pl.ds(rb * 8, 8), cb] = kept.reshape(8, PIECE, BLK)
            row = lax.broadcasted_iota(jnp.int32, (BLK, BLK), 0) + rb * BLK
            col = lax.broadcasted_iota(jnp.int32, (BLK, BLK), 1) + cb * BLK + core * HALF
            diagonal = jnp.where((row == col) & same, F32(0.15), F32(0.0))
            value = (diagonal + F32(0.1275) * kept.astype(F32)) * on
            first[rb // 3, rb % 3, :, pl.ds(cb * BLK, BLK)] = value.astype(BF16)
            mboth[core, pl.ds(rb, 1), pl.ds(cb * BLK, BLK)] = jnp.full((1, BLK), on, F32)
    mask = mboth.at[core]

    pl.semaphore_wait(barrier, len(friends) + jnp.where(turned_self, 0, 1))

    goal = 2 * core + 1 - zl

    def send_first(qc):
        for half in range(2):
            target = me.at(z=goal, core=half)
            src, dst = first.at[half, qc], r1.at[y, zh, qc, half]
            remote(src, dst, i_send.at[half], i_recv.at[zh], target).start()

    def first_sent():
        for half in range(2):
            target = me.at(z=goal, core=half)
            remote(first.at[half], r1.at[y, zh, :, half], i_send.at[half], i_recv.at[zh], target).wait_send()
            remote(mask, mrows.at[zh], m_send.at[half], m_recv.at[zh], target).wait_send()

    for half in range(2):
        remote(mask, mrows.at[zh], m_send.at[half], m_recv.at[zh], me.at(z=goal, core=half)).start()

    def own(who):
        return panel.at[:, z, pl.ds(x * 3, 3), :, pl.ds(pl.multiple_of(who * 128, 128), 128)]

    rows24 = CHUNKS * CLS
    here = pltpu.make_async_copy(adj.at[pl.ds(core * rows24, rows24)], own(core), loc_sem.at[3])
    here.start()
    over = remote(adj.at[pl.ds((1 - core) * rows24, rows24)], own(core), on_send.at[0], on_recv.at[0], sibling)
    go(over)
    go(remote(mask, mask, on_send.at[1], on_recv.at[1], sibling))

    mine = pl.ds(pl.multiple_of(spot * 2 * KEYROWS + core * KEYROWS, KEYROWS), KEYROWS)

    def scatter_keys(waiting=False):
        for block in range(2):
            is_self = turned_self & (zh == block)
            dst = keys.at[zl, x, core]
            if not waiting:
                @pl.when(is_self)
                def _():
                    pltpu.make_async_copy(feat.at[mine], dst, f_recv.at[zl]).start()

            @pl.when(jnp.logical_not(is_self))
            def _():
                device = (block * 4 + x, (zh * 4 + y) * 2 + core)
                copy = remote(feat.at[mine], dst, f_send.at[block], f_recv.at[zl], device)
                if waiting:
                    copy.wait_send()
                else:
                    copy.start()

    here.wait()
    over.wait_recv()

    def a_copy(j, cls, leg, kind):
        sign = 1 if cls % 2 == 0 else -1
        along_x = (cls < X_FIRST[j]) == (leg == 0)
        head = sign if kind != 1 else -sign
        device = ring[("x" if along_x else "z") + ("+" if head == 1 else "-")]
        hop = -sign if kind == 2 else 0
        jc = j * CLS + cls
        if along_x:
            at_x = (x + hop + 8) % 4
            cols = pl.ds(at_x * 3, 3)
            ref = panel.at[jc, z, cols] if leg == 0 else panel.at[jc, :, cols]
        else:
            at_z = (z + hop + 8) % 4
            ref = panel.at[jc, at_z, pl.ds(x * 3, 3)] if leg == 0 else panel.at[jc, at_z]
        step = j * 4 + leg * 2 + (0 if kind == 0 else 1)
        return remote(ref, ref, a_send.at[leg], a_recv.at[step], device)

    def a_stage(j, stage):
        if stage > 0:
            four = pl.ds(j * CLS, CLS)
            ref = {
                1: panel.at[four, 0, pl.ds(0, 3)], 2: panel.at[four, 0, pl.ds(0, 6)],
                3: panel.at[four, 0], 4: panel.at[four, pl.ds(0, 2)],
            }[stage]
            arrived(ref, a_recv.at[j * 4 + stage - 1])
        for cls in range(CLS):
            for kind in ((), (2,), (0, 1), (2,), ())[stage] if stage else (0, 1):
                a_copy(j, cls, stage // 2, kind).start()

    def y_copy(base, cut, k, arriving):
        ref = cut((y - k + 4) % 4 if arriving else y, core)
        return remote(ref, ref, y_send.at[FAMILY[base]], y_recv.at[base * 3 + k - 1], y_peer(k))

    def y_share(base, cut, k):
        ref = cut((y - k + 4) % 4, core)
        remote(ref, ref, s_send.at[FAMILY[base]], s_recv.at[base], sibling).start()

    def y_begin(base, cut, peers=(1, 3, 2)):
        for k in peers:
            y_copy(base, cut, k, False).start()
        y_share(base, cut, 0)

    def y_pass(base, cut, k, relay=None):
        y_copy(base, cut, k, True).wait_recv()
        if relay is not None:
            ref = relay((y - k + 4) % 4, core)
            remote(ref, ref, y_send.at[FAMILY[base]], y_recv.at[base * 3 + 1], y_peer(k)).start()
        y_share(base, cut, k)

    def y_done(base, ref):
        arrived(ref, s_recv.at[base])

    def cut1(a):
        return lambda at_y, who: r1.at[at_y, a, :, who]

    def cut2(q, part, a=slice(None)):
        rows = pl.ds(part[0], part[1])
        return lambda at_y, who: r2.at[at_y, a, q, who, rows]

    def cutk(at_y, who, a=slice(None)):
        return keys.at[a, at_y, who]

    def lhs(q, m, h, kc, part=(0, BLK)):
        pieces = pl.ds(q * 8 + part[0] // PIECE, part[1] // PIECE)
        top = panel[pieces, h, m * 3 + kc].reshape(part[1], 256)
        low = panel[pieces, 2 + h, m * 3 + kc].reshape(part[1], 256)
        return jnp.concatenate([top, low], axis=0)

    def diag(a, q, part):
        row = lax.broadcasted_iota(jnp.int32, (part[1], HALF), 0) + (q * BLK + part[0])
        col = lax.broadcasted_iota(jnp.int32, (part[1], HALF), 1)
        own_block = (1 - zl == a) & (y == x) & (core == zh)
        return jnp.where((row == col) & own_block, F32(0.15), F32(0.0))

    def masked_ranks(a, q, total, part=(0, BLK)):
        keep = mrows[a, pl.ds(core * 3 + q, 1), :] > 0.5
        return jnp.where(keep, diag(a, q, part) + 0.85 * total, 0.0).astype(BF16)

    def sweep_one(q, part):
        size = part[1]

        def body(m, total):
            for h in range(2):
                for kc in range(3):
                    rhs = r1[m, h, kc].reshape(256, HALF)
                    total = total + jnp.dot(lhs(q, m, h, kc, part), rhs, preferred_element_type=F32)
            return total

        total = lax.fori_loop(0, 4, body, jnp.zeros((2 * size, HALF), F32))
        for a in range(2):
            value = masked_ranks(a, q, total[a * size:(a + 1) * size], part)
            r2[y, a, q, core, pl.ds(part[0], size)] = value

    def sweep_two(rows, kc, start):
        for q in rows:
            total = None if start else acc[q]
            for m in range(4):
                for h in range(2):
                    part = jnp.dot(lhs(q, m, h, kc), r2[m, h, kc].reshape(256, HALF), preferred_element_type=F32)
                    total = part if total is None else total + part
            acc[q] = total

    def project(dst, src, first_col, n):
        def body(t, _):
            cols = pl.ds(pl.multiple_of(t * 256, 256), 256)
            w = w_all[:, pl.ds(pl.multiple_of(first_col + t * 256, 256), 256)]
            dst[:, cols] = jnp.dot(src, w, preferred_element_type=F32).astype(BF16)
            return 0

        lax.fori_loop(n, n + 1, body, 0)

    lane = lax.broadcasted_iota(jnp.int32, (BLK, BLK), 1)

    def score_block(t):
        pair, row = t // QC, t % QC
        cols = pl.ds(pl.multiple_of(pair * BLK, BLK), BLK)
        rows = pl.ds(pl.multiple_of(row * BLK, BLK), BLK)
        q2 = query[rows, cols]
        k2 = key_proj[:, cols]
        away = [jnp.where(mboth[c, pl.ds(core * 3 + row, 1), :] > 0.5, F32(0.0), F32(-BIG)) for c in range(2)]
        away = jnp.concatenate(away, axis=1)
        kept = stats[rows, :]
        for side in range(2):
            head = pair * 2 + side
            q1 = jnp.where(lane // HDIM == side, q2, jnp.zeros_like(q2))
            s = lax.dot_general(q1, k2, (((1,), (1,)), ((), ())), preferred_element_type=F32)
            s = s * F32(LOG2E / math.sqrt(HDIM)) + away
            top = jnp.maximum(jnp.max(s, axis=1, keepdims=True), F32(-1e29))
            scores[head, rows, :] = s - top
            kept = jnp.where(lane == HEADS + head, top, kept)
        stats[rows, :] = kept

    def score_blocks(low, high):
        def body(t, _):
            score_block(t)
            return 0

        lax.fori_loop(low, high, body, 0)

    def expo_block(pair, row):
        cols = pl.ds(pl.multiple_of(pair * BLK, BLK), BLK)
        rows = pl.ds(pl.multiple_of(row * BLK, BLK), BLK)
        v2 = value_proj[:, cols]
        spread = bias_in[rows, :]
        both = []
        kept = stats[rows, :]
        for side in range(2):
            head = pair * 2 + side
            bias = (gain[head] * F32(LOG2E)) * jnp.tanh(spread * rate[head])
            e = jnp.exp2(scores[head, rows, :] + bias)
            kept = jnp.where(lane == head, jnp.sum(e, axis=1, keepdims=True), kept)
            both.append(jnp.dot(e.astype(BF16), v2, preferred_element_type=F32))
        stats[rows, :] = kept
        numer[rows, cols] = jnp.where(lane < HDIM, both[0], both[1]).astype(BF16)

    events = []

    def plan(when, what):
        events.append((when, len(events), what))

    def load_weights():
        loads["feat"].wait()
        loads["w"].wait()
        stats[...] = jnp.zeros_like(stats)

    def begin_ranks(base, a):
        pltpu.make_async_copy(first.at[0], r1.at[y, a, :, core], i_recv.at[a]).wait()
        y_begin(base, cut1(a))

    def begin_keys():
        for block in range(2):
            arrived(keys.at[block, y, core], f_recv.at[block])
        y_begin(4, cutk)

    plan(T_LOAD, load_weights)
    for n in range(4):
        plan(T_QUERY[n], lambda n=n: project(query, own_feat[...], 0, n))
        plan(T_KEY[n], lambda n=n: project(key_proj, keys[...].reshape(ROWS, D), D, n))
        plan(T_VALUE[n], lambda n=n: project(value_proj, keys[...].reshape(ROWS, D), 2 * D, n))
    for base, times in ((0, T_OWN), (5, T_FAR)):
        a = base // 5
        plan(times[0], lambda base=base, a=a: begin_ranks(base, a))
        for k, when in zip((1, 3, 2), times[1:]):
            relay = None
            plan(when, lambda base=base, a=a, k=k, relay=relay: y_pass(base, cut1(a), k, relay))
    plan(T_FEAT[0], scatter_keys)
    for qc in range(QC):
        plan(T_FIRST, lambda qc=qc: send_first(qc))
    plan(T_FEAT[1], begin_keys)
    for k, when in zip((1, 3, 2), T_FEAT[2:5]):
        relay = None
        plan(when, lambda k=k, relay=relay: y_pass(4, cutk, k, relay))
    plan(T_FEAT[5], lambda: y_done(4, keys.at[:, :, 0]))
    for j in range(CHUNKS):
        for stage in range(5):
            plan(T_PANEL[stage][j], lambda j=j, stage=stage: a_stage(j, stage))

    def ready():
        y_done(0, r1.at[:, 0, :, 0])
        y_done(5, r1.at[:, 0, :, 0])
        for a in range(2):
            pltpu.make_async_copy(mask, mrows.at[a], m_recv.at[a]).wait()

    plan(T_SCORE[0] - 0.1, lambda: remote(mask, mboth.at[1 - core], on_send.at[1], on_recv.at[1], sibling).wait_recv())
    for n, when in enumerate(T_SCORE):
        plan(when, lambda n=n: score_blocks(2 * n, 2 * n + 2))
    plan(T_READY, ready)
    for base, q, part, when in T_ONE:
        peers = (1, 3) if base in RELAYED else (1, 3, 2)

        def first_sweep(base=base, q=q, part=part, peers=peers):
            sweep_one(q, part)
            y_begin(base, cut2(q, part), peers)

        plan(when, first_sweep)
        for k, late in zip((1, 3, 2), T_LATE[base]):
            relay = cut2(q, part, k // 2) if k != 2 and len(peers) == 2 else None
            plan(late, lambda base=base, q=q, part=part, k=k, relay=relay: y_pass(base, cut2(q, part), k, relay))
        rows = pl.ds(part[0], part[1])
        plan(T_LATE[base][3], lambda base=base, q=q, rows=rows: y_done(base, r2.at[:, :, q, 0, rows]))
    for rows, kc, start, when in T_TWO:
        plan(when, lambda rows=rows, kc=kc, start=start: sweep_two(rows, kc, start))

    def send_weights():
        for k in range(8):
            ref = w_cols.at[spot, core]
            if k == 0:
                remote(w_out_t, ref, w_send.at[1], w_recv.at[1], sibling).start()
            else:
                remote(w_out_t, ref, w_send.at[0], w_recv.at[0], chip(k)[1]).start()
        pltpu.make_async_copy(w_out_t, w_cols.at[spot, core], loc_sem.at[4]).start()

    plan(T_PANEL[3][5] + 0.01, send_weights)
    for _, _, what in sorted(events, key=lambda e: e[:2]):
        what()

    for q in range(QC):
        sweep_two((q,), 2, False)
        for a in range(2):
            staged[a, q] = masked_ranks(a, q, acc[q, a * BLK:(a + 1) * BLK])
        for a in range(2):
            dst = landed.at[zh, q]
            go(remote(staged.at[a, q], dst, o_send.at[2 * q + a], o_recv.at[2 * q + zh], me.at(z=2 * a + 1 - zl)))

    def forward_weights():
        pltpu.make_async_copy(w_out_t, w_cols.at[spot, core], loc_sem.at[4]).wait()
        arrived(w_cols.at[pl.ds(0, 7), 0], w_recv.at[0])
        for k in range(1, 8):
            ref = w_cols.at[(spot + k) % 8, core]
            remote(ref, ref, w_send.at[1], w_recv.at[1], sibling).start()

    def widen(ref, half, q):
        cols = pl.ds(half * HALF, HALF)
        bias_in[pl.ds(q * BLK, BLK), cols] = ref[q].astype(F32) * F32(math.sqrt(NODES))

    def owned(q, at):
        return pl.ds(pl.multiple_of(q * BLK + at * OWNROWS, OWNROWS), OWNROWS)

    def attend(q):
        for half in range(2):
            arrived(landed.at[half, q], o_recv.at[2 * q + half])
            widen(landed.at[half], half, q)

        def body(t, _):
            expo_block(t, q)
            return 0

        lax.fori_loop(0, HEADS // 2, body, 0)
        for k in range(1, 8):
            other, device = chip(k)
            rows = owned(q, other)
            remote(numer.at[rows], numer_all.at[spot, q], n_send.at[0], n_recv.at[q], device).start()
            remote(stats.at[rows], stats_all.at[spot, q], t_send.at[0], t_recv.at[q], device).start()
        numer_all[spot, q] = numer[owned(q, spot), :]
        stats_all[spot, q] = stats[owned(q, spot), :]

    low = lax.broadcasted_iota(jnp.int32, (OWNROWS, BLK), 1) < HDIM

    def combine(q):
        arrived(stats_all.at[pl.ds(0, 7), q], t_recv.at[q])
        arrived(numer_all.at[pl.ds(0, 7), q], n_recv.at[q])
        table = [stats_all[s, q] for s in range(8)]
        tops = [t[:, HEADS:2 * HEADS] for t in table]
        peak = tops[0]
        for t in tops[1:]:
            peak = jnp.maximum(peak, t)
        weights = [jnp.exp2(t - peak) for t in tops]
        total = weights[0] * table[0][:, :HEADS]
        for s in range(1, 8):
            total = total + weights[s] * table[s][:, :HEADS]
        weights = [w / total for w in weights]
        for pair in range(HEADS // 2):
            cols = pl.ds(pair * BLK, BLK)
            value = jnp.zeros((OWNROWS, BLK), F32)
            for s in range(8):
                w = jnp.where(low, weights[s][:, 2 * pair:2 * pair + 1], weights[s][:, 2 * pair + 1:2 * pair + 2])
                value = value + w * numer_all[s, q, :, cols].astype(F32)
            att[q, :, cols] = value.astype(BF16)

    for q in range(QC):
        attend(q)
    forward_weights()
    for q in range(QC):
        combine(q)

    arrived(w_cols.at[:, 0], w_recv.at[1])
    mixed = lax.dot_general(
        att[...].reshape(KEYROWS, D), w_cols[...].reshape(D, D), (((1,), (1,)), ((), ())), preferred_element_type=F32
    ).astype(BF16)
    for c in range(2 * 8):
        mix[c // 2, c % 2] = mixed[:, c * HDIM:(c + 1) * HDIM].reshape(QC, OWNROWS, HDIM)

    def rows_of(who, at):
        return out.at[who, :, pl.ds(pl.multiple_of(at * OWNROWS, OWNROWS), OWNROWS)]

    for k in range(8):
        for flip in range(2):
            if k == 0 and flip == 0:
                continue
            other, device = chip(k, (core + flip) % 2)
            src = mix.at[other, (core + flip) % 2]
            remote(src, rows_of(core, spot), x_send.at[flip], x_recv.at[flip], device).start()
    last = pltpu.make_async_copy(mix.at[spot, core], rows_of(core, spot), loc_sem.at[5])
    last.start()
    for flip in range(2):
        arrived(mix.at[pl.ds(0, 7 + flip), 0], x_recv.at[flip])
    last.wait()
    for send in sends:
        send.wait_send()
    for flip in range(2):
        arrived(mix.at[pl.ds(0, 7 + flip), 0], x_send.at[flip])
        arrived(w_cols.at[pl.ds(0, 7 + flip), 0], w_send.at[flip])
    arrived(panel.at[:, 0, pl.ds(0, 9)], a_send.at[0])
    arrived(panel.at[:, pl.ds(0, 3)], a_send.at[1])
    three = pl.ds(0, 3)
    for n, ref in enumerate((r1.at[three, :, :, 0], r2.at[three, :, :, 0], keys.at[:, three, 0])):
        arrived(ref, y_send.at[n])
    for n, ref in enumerate((r1.at[:, :, :, 0], r2.at[:, :, :, 0], keys.at[:, :, 0])):
        arrived(ref, s_send.at[n])
    arrived(numer_all.at[pl.ds(0, 7)], n_send.at[0])
    arrived(stats_all.at[pl.ds(0, 7)], t_send.at[0])
    first_sent()

    scatter_keys(waiting=True)


def shards(node_features, edge_weight, pattern, w_qkv, w_out, bias_gain, bias_rate):
    dma = pltpu.SemaphoreType.DMA
    anywhere = pl.BlockSpec(memory_space=pl.ANY)
    vmem = pl.BlockSpec(memory_space=pltpu.VMEM)
    smem = pl.BlockSpec(memory_space=pltpu.SMEM)
    counts = (2, 4 * CHUNKS, 2, 2, 2, 2, 2, 2, 3, 21, 3, 7, 2, 2, 6, 6, 1, QC, 1, QC, 2, 2, 2, 2)
    sems = [dma((n,)) for n in counts]
    mixed = pl.pallas_call(
        fused_kernel,
        name="fused",
        out_shape=jax.ShapeDtypeStruct((2, QC, BLK, HDIM), BF16),
        in_specs=[anywhere, smem, anywhere, anywhere, anywhere, smem, smem],
        out_specs=vmem,
        scratch_shapes=[
            pltpu.VMEM((CHUNKS * CLS, 4, 12, PIECE, 256), BF16),
            pltpu.VMEM((4, 2, QC, 2, BLK, HALF), BF16),
            pltpu.VMEM((4, 2, QC, 2, BLK, HALF), BF16),
            pltpu.VMEM((QC, 2 * BLK, HALF), F32),
            pltpu.VMEM((2, QC, BLK, HALF), BF16),
            pltpu.VMEM((2, QC, BLK, HALF), BF16),
            pltpu.VMEM((2 * CHUNKS * CLS, 3, PIECE, BLK), BF16),
            pltpu.VMEM((2, QC, BLK, HALF), BF16),
            pltpu.VMEM((2, 8, HALF), F32),
            pltpu.VMEM((2, 8, HALF), F32),
            pltpu.VMEM((2, 4, 2, KEYROWS, D), BF16),
            pltpu.VMEM((HALF, D), BF16),
            pltpu.VMEM((D, 3 * D), BF16),
            pltpu.VMEM((ROWS, HALF), BF16),
            pltpu.VMEM((HALF, D), BF16),
            pltpu.VMEM((ROWS, D), BF16),
            pltpu.VMEM((ROWS, D), BF16),
            pltpu.VMEM((HEADS, HALF, ROWS), F32),
            pltpu.VMEM((HALF, ROWS), F32),
            pltpu.VMEM((HALF, D), BF16),
            pltpu.VMEM((8, QC, OWNROWS, D), BF16),
            pltpu.VMEM((HALF, BLK), F32),
            pltpu.VMEM((8, QC, OWNROWS, BLK), F32),
            pltpu.VMEM((QC, OWNROWS, D), BF16),
            pltpu.VMEM((8, 2, HDIM, D), BF16),
            pltpu.VMEM((8, 2, QC, OWNROWS, HDIM), BF16),
            dma((6,)),
            *sems,
        ],
        compiler_params=pltpu.CompilerParams(
            collective_id=0, has_side_effects=True, vmem_limit_bytes=65 * 1000 * 1000
        ),
    )(edge_weight, pattern.T, node_features, w_qkv, w_out.T, bias_gain, bias_rate)
    return mixed.reshape(ROWS, HDIM)


def solution(mesh):
    in_specs = (P("row", None), P("row", "col"), P("row", "col"), P(), P(None, "col"), P(), P())
    return jax.shard_map(shards, mesh=mesh, in_specs=in_specs, out_specs=P("row", "col"), check_vma=False)
```

time: 160 us -> 129 us (0.81)
  the two profiles are of different devices: /device:TPU:1 before, /device:TPU:9 now
where the time goes in v3:
time: 129 us; the launch traced here: 128 us
  Pallas kernels  127 us (98%)
  local copies, waits for them, and re-layouts  1.69 us (1%)
    pallas_call x1, Pallas kernels, shards(): pl.pallas_call(fused_kernel, name='fused', out_shape=jax.ShapeDtypeStruct...  127 us

profile of v3, /device:TPU:9, one launch (start us, length us, event | category | flops | bytes accessed | tf_op | source)
XLA Modules:
  0.0 128.4 jit_solution(9387147743490010694)
XLA Ops:
  0.0 126.7 %fused.1 = bf16[2,3,128,64]{3,2,1,0:T(8,128)(2,1)} custom-call(bf16[768,384]{1,0:T(8,128)(2,1)} %edge.1, s32[3,6]{1,0:T(4,128)} %bitcast.5, bf16[768,1024]{1,0:T(8,128)(2,1)} %feat.1, bf16[1024,3072]{1,0:T(8,128)(2,1)} %w_qkv.1, bf16[64,1024]{1,0:T(8,128)(2,1)} %bitcast.4, f32[16]{0:T(128)} %gain.1, f32[16]{0:T(128)} %rate.1), custom_call_target="tpu_custom_call" | custom-call | tf_op jit(solution)/shard_map/fused/pallas_call | solution.py:560
  126.8 1.7 %copy.8 = bf16[768,64]{0,1:T(8,128)(2,1)} copy(bf16[768,64]{1,0:T(8,128)(2,1)} %bitcast.3) | data formatting | bytes 196608 | tf_op jit(solution)/shard_map/reshape | solution.py:600

commit v4 on v3

--- a/solution.py
+++ b/solution.py
@@ -18,34 +18,34 @@
 CHUNKS = 6
 CLS = 4
 X_FIRST = (2, 2, 2, 2, 2, 2)
-RELAYED = ()
-T_LOAD = 2.9
-T_QUERY = (4.5, 3.5, 3.0, 4.0)
-T_KEY = (27.5, 26.5, 25.0, 27.0)
-T_VALUE = (29.5, 28.0, 33.5, 29.0)
-T_FIRST = 0.0
-T_OWN = (5.0, 11.5, 12.0, 13.5)
-T_FAR = (5.5, 16.0, 15.5, 18.5)
-T_FEAT = (2.5, 7.0, 21.5, 21.0, 23.5, 24.5)
+RELAYED = (0, 1, 2, 4, 5)
+T_LOAD = 3.9
+T_QUERY = (5.0, 4.0, 5.5, 4.5)
+T_KEY = (23.5, 19.5, 21.0, 22.0)
+T_VALUE = (18.5, 20.0, 20.5, 36.5)
+T_FIRST = (0.0, 1.0, 1.5)
+T_OWN = (6.5, 14.0, 14.5, 23.0)
+T_FAR = (7.0, 17.0, 16.5, 22.5)
+T_FEAT = (0.5, 6.0, 12.0, 11.5, 17.5, 18.0)
 T_PANEL = (
-    (0.5, 1.0, 1.5, 2.0, 9.0, 10.0),
-    (6.0, 6.5, 7.5, 8.0, 13.0, 14.5),
-    (8.5, 9.5, 10.5, 11.0, 18.0, 20.5),
-    (12.5, 14.0, 16.5, 17.0, 24.0, 28.5),
-    (17.5, 19.5, 22.0, 22.5, 30.0, 34.0),
+    (2.0, 2.5, 3.0, 3.5, 10.0, 11.0),
+    (7.5, 8.0, 8.5, 9.0, 15.0, 16.0),
+    (9.5, 10.5, 12.5, 13.0, 25.0, 28.5),
+    (13.5, 15.5, 19.0, 21.5, 34.5, 37.0),
+    (24.0, 27.5, 30.0, 31.5, 38.5, 41.0),
 )
-T_SCORE = (35.5, 36.0, 37.0, 38.5, 39.0, 41.0, 42.5, 43.5, 44.0, 44.5, 45.0, 46.0)
-T_READY = 19.0
+T_SCORE = (24.5, 26.0, 27.0, 29.0, 29.5, 30.5, 31.0, 32.5, 33.0, 33.5, 34.0, 36.0)
+T_READY = 26.5
 T_ONE = (
-    (1, 0, (0, 128), 20.0), (2, 1, (0, 128), 23.0), (3, 2, (0, 64), 31.0), (6, 2, (64, 64), 34.5)
+    (1, 0, (0, 128), 28.0), (2, 1, (0, 128), 32.0), (3, 2, (0, 64), 39.0), (6, 2, (64, 64), 41.5)
 )
 T_LATE = {
-    1: (26.0, 25.5, 30.5, 31.5),
-    2: (32.5, 33.0, 36.5, 39.5),
-    3: (38.0, 37.5, 40.5, 43.0),
-    6: (42.0, 41.5, 45.5, 46.5),
+    1: (35.5, 35.0, 39.5, 40.0),
+    2: (37.5, 38.0, 42.5, 44.0),
+    3: (43.0, 43.5, 45.0, 46.5),
+    6: (46.0, 45.5, 47.0, 47.5),
 }
-T_TWO = (((0, 1), 0, True, 32.0), ((2,), 0, True, 35.0), ((0, 1, 2), 1, False, 40.0))
+T_TWO = (((0, 1), 0, True, 40.5), ((2,), 0, True, 42.0), ((0, 1, 2), 1, False, 44.5))
 FAMILY = (0, 1, 1, 1, 2, 0, 1)
 PIECE = 16
 KEYROWS = 48
@@ -81,7 +81,7 @@
 
 def fused_kernel(
     edge, pattern, feat, w_qkv, w_out_t, gain, rate, out,
-    panel, r1, r2, acc, staged, landed, adj, first, mrows, mboth, keys, own_feat, w_all, edge_v,
+    panel, r1, r2, acc, staged, landed, adj, first, mrows, mboth, first_sib, keys, own_feat, w_all, edge_v,
     query, key_proj, value_proj, scores, bias_in, numer, numer_all, stats, stats_all, att, w_cols, mix,
     loc_sem, a_send, a_recv, on_send, on_recv, i_send, i_recv, m_send, m_recv,
     y_send, y_recv, s_send, s_recv, f_send, f_recv, o_send, o_recv,
@@ -156,17 +156,23 @@
 
     goal = 2 * core + 1 - zl
 
+    def first_copy(qc, mine):
+        src = first.at[core, qc] if mine else first_sib.at[qc]
+        way = core if mine else 1 - core
+        dst = r1.at[y, zh, qc, core]
+        return remote(src, dst, i_send.at[0 if mine else 1], i_recv.at[zh], me.at(z=2 * way + 1 - zl))
+
     def send_first(qc):
+        if qc == 0:
+            arrived(first_sib, on_recv.at[2])
+        for mine in (True, False):
+            first_copy(qc, mine).start()
+
+    def first_sent():
+        for n in range(2):
+            arrived(first.at[0], i_send.at[n])
         for half in range(2):
-            target = me.at(z=goal, core=half)
-            src, dst = first.at[half, qc], r1.at[y, zh, qc, half]
-            remote(src, dst, i_send.at[half], i_recv.at[zh], target).start()
-
-    def first_sent():
-        for half in range(2):
-            target = me.at(z=goal, core=half)
-            remote(first.at[half], r1.at[y, zh, :, half], i_send.at[half], i_recv.at[zh], target).wait_send()
-            remote(mask, mrows.at[zh], m_send.at[half], m_recv.at[zh], target).wait_send()
+            remote(mask, mrows.at[zh], m_send.at[half], m_recv.at[zh], me.at(z=goal, core=half)).wait_send()
 
     for half in range(2):
         remote(mask, mrows.at[zh], m_send.at[half], m_recv.at[zh], me.at(z=goal, core=half)).start()
@@ -179,6 +185,7 @@
     here.start()
     over = remote(adj.at[pl.ds((1 - core) * rows24, rows24)], own(core), on_send.at[0], on_recv.at[0], sibling)
     go(over)
+    go(remote(first.at[1 - core], first_sib, on_send.at[2], on_recv.at[2], sibling))
     go(remote(mask, mask, on_send.at[1], on_recv.at[1], sibling))
 
     mine = pl.ds(pl.multiple_of(spot * 2 * KEYROWS + core * KEYROWS, KEYROWS), KEYROWS)
@@ -285,14 +292,13 @@
     def sweep_one(q, part):
         size = part[1]
 
-        def body(m, total):
+        total = None
+        for m in range(4):
             for h in range(2):
                 for kc in range(3):
                     rhs = r1[m, h, kc].reshape(256, HALF)
-                    total = total + jnp.dot(lhs(q, m, h, kc, part), rhs, preferred_element_type=F32)
-            return total
-
-        total = lax.fori_loop(0, 4, body, jnp.zeros((2 * size, HALF), F32))
+                    product = jnp.dot(lhs(q, m, h, kc, part), rhs, preferred_element_type=F32)
+                    total = product if total is None else total + product
         for a in range(2):
             value = masked_ranks(a, q, total[a * size:(a + 1) * size], part)
             r2[y, a, q, core, pl.ds(part[0], size)] = value
@@ -371,12 +377,12 @@
 
     def begin_ranks(base, a):
         pltpu.make_async_copy(first.at[0], r1.at[y, a, :, core], i_recv.at[a]).wait()
-        y_begin(base, cut1(a))
+        y_begin(base, cut1(a), (1, 3) if base in RELAYED else (1, 3, 2))
 
     def begin_keys():
         for block in range(2):
             arrived(keys.at[block, y, core], f_recv.at[block])
-        y_begin(4, cutk)
+        y_begin(4, cutk, (1, 3) if 4 in RELAYED else (1, 3, 2))
 
     plan(T_LOAD, load_weights)
     for n in range(4):
@@ -387,14 +393,16 @@
         a = base // 5
         plan(times[0], lambda base=base, a=a: begin_ranks(base, a))
         for k, when in zip((1, 3, 2), times[1:]):
-            relay = None
+            relay = cut1(a) if base in RELAYED and k == 1 + 2 * a else None
             plan(when, lambda base=base, a=a, k=k, relay=relay: y_pass(base, cut1(a), k, relay))
     plan(T_FEAT[0], scatter_keys)
     for qc in range(QC):
-        plan(T_FIRST, lambda qc=qc: send_first(qc))
+        plan(T_FIRST[qc], lambda qc=qc: send_first(qc))
     plan(T_FEAT[1], begin_keys)
     for k, when in zip((1, 3, 2), T_FEAT[2:5]):
         relay = None
+        if 4 in RELAYED and k != 2:
+            relay = lambda at_y, who, k=k: cutk(at_y, who, k // 2)
         plan(when, lambda k=k, relay=relay: y_pass(4, cutk, k, relay))
     plan(T_FEAT[5], lambda: y_done(4, keys.at[:, :, 0]))
     for j in range(CHUNKS):
@@ -555,7 +563,7 @@
     anywhere = pl.BlockSpec(memory_space=pl.ANY)
     vmem = pl.BlockSpec(memory_space=pltpu.VMEM)
     smem = pl.BlockSpec(memory_space=pltpu.SMEM)
-    counts = (2, 4 * CHUNKS, 2, 2, 2, 2, 2, 2, 3, 21, 3, 7, 2, 2, 6, 6, 1, QC, 1, QC, 2, 2, 2, 2)
+    counts = (2, 4 * CHUNKS, 3, 3, 2, 2, 2, 2, 3, 21, 3, 7, 2, 2, 6, 6, 1, QC, 1, QC, 2, 2, 2, 2)
     sems = [dma((n,)) for n in counts]
     mixed = pl.pallas_call(
         fused_kernel,
@@ -574,6 +582,7 @@
             pltpu.VMEM((2, QC, BLK, HALF), BF16),
             pltpu.VMEM((2, 8, HALF), F32),
             pltpu.VMEM((2, 8, HALF), F32),
+            pltpu.VMEM((QC, BLK, HALF), BF16),
             pltpu.VMEM((2, 4, 2, KEYROWS, D), BF16),
             pltpu.VMEM((HALF, D), BF16),
             pltpu.VMEM((D, 3 * D), BF16),

time: 129 us -> 122 us (0.946)
  the two profiles are of different devices: /device:TPU:9 before, /device:TPU:1 now
where the time goes in v4:
time: 122 us; the launch traced here: 121 us
  Pallas kernels  120 us (98%)
  local copies, waits for them, and re-layouts  1.69 us (1%)
    pallas_call x1, Pallas kernels, shards(): pl.pallas_call(fused_kernel, name='fused', out_shape=jax.ShapeDtypeStruct...  120 us

profile of v4, /device:TPU:1, one launch (start us, length us, event | category | flops | bytes accessed | tf_op | source)
XLA Modules:
  0.0 121.4 jit_solution(8189782975516100303)
XLA Ops:
  0.0 119.7 %fused.1 = bf16[2,3,128,64]{3,2,1,0:T(8,128)(2,1)} custom-call(bf16[768,384]{1,0:T(8,128)(2,1)} %edge.1, s32[3,6]{1,0:T(4,128)} %bitcast.5, bf16[768,1024]{1,0:T(8,128)(2,1)} %feat.1, bf16[1024,3072]{1,0:T(8,128)(2,1)} %w_qkv.1, bf16[64,1024]{1,0:T(8,128)(2,1)} %bitcast.4, f32[16]{0:T(128)} %gain.1, f32[16]{0:T(128)} %rate.1), custom_call_target="tpu_custom_call" | custom-call | tf_op jit(solution)/shard_map/fused/pallas_call | solution.py:568
  119.7 1.7 %copy.8 = bf16[768,64]{0,1:T(8,128)(2,1)} copy(bf16[768,64]{1,0:T(8,128)(2,1)} %bitcast.3) | data formatting | bytes 196608 | tf_op jit(solution)/shard_map/reshape | solution.py:609

commit v5 on v4

--- a/solution.py
+++ b/solution.py
@@ -435,14 +435,20 @@
     for rows, kc, start, when in T_TWO:
         plan(when, lambda rows=rows, kc=kc, start=start: sweep_two(rows, kc, start))
 
+    quarter = pl.ds(pl.multiple_of(y * 256, 256), 256)
+
     def send_weights():
-        for k in range(8):
-            ref = w_cols.at[spot, core]
-            if k == 0:
-                remote(w_out_t, ref, w_send.at[1], w_recv.at[1], sibling).start()
-            else:
-                remote(w_out_t, ref, w_send.at[0], w_recv.at[0], chip(k)[1]).start()
-        pltpu.make_async_copy(w_out_t, w_cols.at[spot, core], loc_sem.at[4]).start()
+        src, dst = w_out_t.at[:, quarter], w_cols.at[spot, core, :, quarter]
+        for k in range(1, 8):
+            remote(src, dst, w_send.at[0], w_recv.at[0], chip(k)[1]).start()
+        pltpu.make_async_copy(src, dst, loc_sem.at[4]).start()
+
+    def cross_weights():
+        ref = w_cols.at[:, core, :, quarter]
+        arrived(w_cols.at[spot, core, :, quarter], loc_sem.at[4])
+        arrived(w_cols.at[pl.ds(0, 7), 0, :, pl.ds(0, 256)], w_recv.at[0])
+        for k in (1, 3, 2):
+            remote(ref, ref, w_send.at[2], w_recv.at[2], y_peer(k)).start()
 
     plan(T_PANEL[3][5] + 0.01, send_weights)
     for _, _, what in sorted(events, key=lambda e: e[:2]):
@@ -456,12 +462,12 @@
             dst = landed.at[zh, q]
             go(remote(staged.at[a, q], dst, o_send.at[2 * q + a], o_recv.at[2 * q + zh], me.at(z=2 * a + 1 - zl)))
 
+    cross_weights()
+
     def forward_weights():
-        pltpu.make_async_copy(w_out_t, w_cols.at[spot, core], loc_sem.at[4]).wait()
-        arrived(w_cols.at[pl.ds(0, 7), 0], w_recv.at[0])
-        for k in range(1, 8):
-            ref = w_cols.at[(spot + k) % 8, core]
-            remote(ref, ref, w_send.at[1], w_recv.at[1], sibling).start()
+        arrived(w_cols.at[:, 0, :, pl.ds(0, 768)], w_recv.at[2])
+        ref = w_cols.at[:, core]
+        remote(ref, ref, w_send.at[1], w_recv.at[1], sibling).start()
 
     def widen(ref, half, q):
         cols = pl.ds(half * HALF, HALF)
@@ -543,9 +549,11 @@
         send.wait_send()
     for flip in range(2):
         arrived(mix.at[pl.ds(0, 7 + flip), 0], x_send.at[flip])
-        arrived(w_cols.at[pl.ds(0, 7 + flip), 0], w_send.at[flip])
     arrived(panel.at[:, 0, pl.ds(0, 9)], a_send.at[0])
     arrived(panel.at[:, pl.ds(0, 3)], a_send.at[1])
+    arrived(w_cols.at[pl.ds(0, 7), 0, :, pl.ds(0, 256)], w_send.at[0])
+    arrived(w_cols.at[:, 0], w_send.at[1])
+    arrived(w_cols.at[:, 0, :, pl.ds(0, 768)], w_send.at[2])
     three = pl.ds(0, 3)
     for n, ref in enumerate((r1.at[three, :, :, 0], r2.at[three, :, :, 0], keys.at[:, three, 0])):
         arrived(ref, y_send.at[n])
@@ -563,7 +571,7 @@
     anywhere = pl.BlockSpec(memory_space=pl.ANY)
     vmem = pl.BlockSpec(memory_space=pltpu.VMEM)
     smem = pl.BlockSpec(memory_space=pltpu.SMEM)
-    counts = (2, 4 * CHUNKS, 3, 3, 2, 2, 2, 2, 3, 21, 3, 7, 2, 2, 6, 6, 1, QC, 1, QC, 2, 2, 2, 2)
+    counts = (2, 4 * CHUNKS, 3, 3, 2, 2, 2, 2, 3, 21, 3, 7, 2, 2, 6, 6, 1, QC, 1, QC, 3, 3, 2, 2)
     sems = [dma((n,)) for n in counts]
     mixed = pl.pallas_call(
         fused_kernel,

time: 122 us -> 114 us (0.934)
  Pallas kernels: 120 us -> 113 us
    pallas_call x1, Pallas kernels: 120 us -> 113 us  [shards(): pl.pallas_call(fused_kernel, name='fused', out_shape=jax.ShapeDtypeStruct...]
where the time goes in v5:
time: 114 us
  Pallas kernels  113 us (99%)
  local copies, waits for them, and re-layouts  1.69 us (1%)
    pallas_call x1, Pallas kernels, shards(): pl.pallas_call(fused_kernel, name='fused', out_shape=jax.ShapeDtypeStruct...  113 us

profile of v5, /device:TPU:1, one launch (start us, length us, event | category | flops | bytes accessed | tf_op | source)
XLA Modules:
  0.0 114.2 jit_solution(10154517988951152259)
XLA Ops:
  0.0 112.5 %fused.1 = bf16[2,3,128,64]{3,2,1,0:T(8,128)(2,1)} custom-call(bf16[768,384]{1,0:T(8,128)(2,1)} %edge.1, s32[3,6]{1,0:T(4,128)} %bitcast.5, bf16[768,1024]{1,0:T(8,128)(2,1)} %feat.1, bf16[1024,3072]{1,0:T(8,128)(2,1)} %w_qkv.1, bf16[64,1024]{1,0:T(8,128)(2,1)} %bitcast.4, f32[16]{0:T(128)} %gain.1, f32[16]{0:T(128)} %rate.1), custom_call_target="tpu_custom_call" | custom-call | tf_op jit(solution)/shard_map/fused/pallas_call | solution.py:576
  112.5 1.7 %copy.8 = bf16[768,64]{0,1:T(8,128)(2,1)} copy(bf16[768,64]{1,0:T(8,128)(2,1)} %bitcast.3) | data formatting | bytes 196608 | tf_op jit(solution)/shard_map/reshape | solution.py:617

commit v6 on v5

--- a/solution.py
+++ b/solution.py
@@ -24,9 +24,9 @@
 T_KEY = (23.5, 19.5, 21.0, 22.0)
 T_VALUE = (18.5, 20.0, 20.5, 36.5)
 T_FIRST = (0.0, 1.0, 1.5)
-T_OWN = (6.5, 14.0, 14.5, 23.0)
-T_FAR = (7.0, 17.0, 16.5, 22.5)
-T_FEAT = (0.5, 6.0, 12.0, 11.5, 17.5, 18.0)
+T_OWN = (9.7, 14.0, 14.5, 23.0)
+T_FAR = (9.8, 17.0, 16.5, 22.5)
+T_FEAT = (0.5, 9.6, 12.0, 11.5, 17.5, 18.0)
 T_PANEL = (
     (2.0, 2.5, 3.0, 3.5, 10.0, 11.0),
     (7.5, 8.0, 8.5, 9.0, 15.0, 16.0),

time: 114 us -> 118 us (1.035)
  Pallas kernels: 113 us -> 116 us
    pallas_call x1, Pallas kernels: 113 us -> 116 us  [shards(): pl.pallas_call(fused_kernel, name='fused', out_shape=jax.ShapeDtypeStruct...]
where the time goes in v6:
time: 118 us
  Pallas kernels  116 us (98%)
  local copies, waits for them, and re-layouts  1.69 us (1%)
    pallas_call x1, Pallas kernels, shards(): pl.pallas_call(fused_kernel, name='fused', out_shape=jax.ShapeDtypeStruct...  116 us

profile of v6, /device:TPU:1, one launch (start us, length us, event | category | flops | bytes accessed | tf_op | source)
XLA Modules:
  0.0 117.9 jit_solution(13038420225759907567)
XLA Ops:
  0.0 116.2 %fused.1 = bf16[2,3,128,64]{3,2,1,0:T(8,128)(2,1)} custom-call(bf16[768,384]{1,0:T(8,128)(2,1)} %edge.1, s32[3,6]{1,0:T(4,128)} %bitcast.5, bf16[768,1024]{1,0:T(8,128)(2,1)} %feat.1, bf16[1024,3072]{1,0:T(8,128)(2,1)} %w_qkv.1, bf16[64,1024]{1,0:T(8,128)(2,1)} %bitcast.4, f32[16]{0:T(128)} %gain.1, f32[16]{0:T(128)} %rate.1), custom_call_target="tpu_custom_call" | custom-call | tf_op jit(solution)/shard_map/fused/pallas_call | solution.py:576
  116.3 1.7 %copy.8 = bf16[768,64]{0,1:T(8,128)(2,1)} copy(bf16[768,64]{1,0:T(8,128)(2,1)} %bitcast.3) | data formatting | bytes 196608 | tf_op jit(solution)/shard_map/reshape | solution.py:617

commit v7 on v6

--- a/solution.py
+++ b/solution.py
@@ -20,30 +20,30 @@
 X_FIRST = (2, 2, 2, 2, 2, 2)
 RELAYED = (0, 1, 2, 4, 5)
 T_LOAD = 3.9
-T_QUERY = (5.0, 4.0, 5.5, 4.5)
-T_KEY = (23.5, 19.5, 21.0, 22.0)
-T_VALUE = (18.5, 20.0, 20.5, 36.5)
-T_FIRST = (0.0, 1.0, 1.5)
-T_OWN = (9.7, 14.0, 14.5, 23.0)
-T_FAR = (9.8, 17.0, 16.5, 22.5)
-T_FEAT = (0.5, 9.6, 12.0, 11.5, 17.5, 18.0)
+T_QUERY = (5.5, 4.0, 5.0, 4.5)
+T_KEY = (21.5, 21.0, 20.5, 19.0)
+T_VALUE = (19.5, 23.5, 36.5, 24.5)
+T_FIRST = (0.0, 3.0, 3.5)
+T_OWN = (9.0, 17.0, 16.5, 24.0)
+T_FAR = (8.5, 14.5, 15.0, 23.0)
+T_FEAT = (0.5, 8.0, 13.0, 12.5, 18.0, 18.5)
 T_PANEL = (
-    (2.0, 2.5, 3.0, 3.5, 10.0, 11.0),
-    (7.5, 8.0, 8.5, 9.0, 15.0, 16.0),
-    (9.5, 10.5, 12.5, 13.0, 25.0, 28.5),
-    (13.5, 15.5, 19.0, 21.5, 34.5, 37.0),
-    (24.0, 27.5, 30.0, 31.5, 38.5, 41.0),
+    (1.0, 1.5, 2.0, 2.5, 10.0, 11.0),
+    (6.0, 6.5, 7.0, 7.5, 14.0, 16.0),
+    (9.5, 10.5, 11.5, 12.0, 22.0, 26.5),
+    (13.5, 15.5, 17.5, 20.0, 33.0, 37.0),
+    (22.5, 25.5, 28.0, 30.0, 38.5, 41.0),
 )
-T_SCORE = (24.5, 26.0, 27.0, 29.0, 29.5, 30.5, 31.0, 32.5, 33.0, 33.5, 34.0, 36.0)
-T_READY = 26.5
+T_SCORE = (26.0, 28.5, 29.0, 29.5, 31.0, 31.5, 32.0, 32.5, 33.5, 35.0, 35.5, 36.0)
+T_READY = 27.0
 T_ONE = (
-    (1, 0, (0, 128), 28.0), (2, 1, (0, 128), 32.0), (3, 2, (0, 64), 39.0), (6, 2, (64, 64), 41.5)
+    (1, 0, (0, 128), 27.5), (2, 1, (0, 128), 30.5), (3, 2, (0, 64), 39.0), (6, 2, (64, 64), 41.5)
 )
 T_LATE = {
-    1: (35.5, 35.0, 39.5, 40.0),
-    2: (37.5, 38.0, 42.5, 44.0),
-    3: (43.0, 43.5, 45.0, 46.5),
-    6: (46.0, 45.5, 47.0, 47.5),
+    1: (34.5, 34.0, 39.5, 40.0),
+    2: (38.0, 37.5, 42.5, 44.0),
+    3: (43.5, 43.0, 45.0, 46.5),
+    6: (45.5, 46.0, 47.0, 47.5),
 }
 T_TWO = (((0, 1), 0, True, 40.5), ((2,), 0, True, 42.0), ((0, 1, 2), 1, False, 44.5))
 FAMILY = (0, 1, 1, 1, 2, 0, 1)

time: 118 us -> 116 us (0.983)
  Pallas kernels: 116 us -> 114 us
    pallas_call x1, Pallas kernels: 116 us -> 114 us  [shards(): pl.pallas_call(fused_kernel, name='fused', out_shape=jax.ShapeDtypeStruct...]
where the time goes in v7:
time: 116 us; the launch traced here: 115 us
  Pallas kernels  114 us (98%)
  local copies, waits for them, and re-layouts  1.69 us (1%)
    pallas_call x1, Pallas kernels, shards(): pl.pallas_call(fused_kernel, name='fused', out_shape=jax.ShapeDtypeStruct...  114 us

profile of v7, /device:TPU:1, one launch (start us, length us, event | category | flops | bytes accessed | tf_op | source)
XLA Modules:
  0.0 115.5 jit_solution(1801955261405470767)
XLA Ops:
  0.0 113.8 %fused.1 = bf16[2,3,128,64]{3,2,1,0:T(8,128)(2,1)} custom-call(bf16[768,384]{1,0:T(8,128)(2,1)} %edge.1, s32[3,6]{1,0:T(4,128)} %bitcast.5, bf16[768,1024]{1,0:T(8,128)(2,1)} %feat.1, bf16[1024,3072]{1,0:T(8,128)(2,1)} %w_qkv.1, bf16[64,1024]{1,0:T(8,128)(2,1)} %bitcast.4, f32[16]{0:T(128)} %gain.1, f32[16]{0:T(128)} %rate.1), custom_call_target="tpu_custom_call" | custom-call | tf_op jit(solution)/shard_map/fused/pallas_call | solution.py:576
  113.8 1.7 %copy.8 = bf16[768,64]{0,1:T(8,128)(2,1)} copy(bf16[768,64]{1,0:T(8,128)(2,1)} %bitcast.3) | data formatting | bytes 196608 | tf_op jit(solution)/shard_map/reshape | solution.py:617
